TPU v7x, 256 devices: a whole 4x4x8 slice. The times are simulated.
256 devices in a mesh: gx: 8 (over y_hi, x), gy: 4 (over y_lo, core), ta: 8 (over z).
Axes of the slice: x: 4, y: 4 (y_hi: 2, y_lo: 2; y = y_hi * 2 + y_lo), z: 8, core: 2. Of those that a mesh axis runs over, the one named last changes fastest.
Arguments:
- displacement: float32 [3, 64, 32, 256], P(None, 'gx', 'gy'), may hold values from -3 to 3
- pressure: float32 [64, 32, 256], P('gx', 'gy'), may hold values from -6 to 6
- porosity: float32 [64, 32, 256], P('gx', 'gy'), may hold values from 0.1 to 0.3
- labels: int32 [64, 32, 256], P('gx', 'gy'), may hold values from 0 to 5
- ventricle_mask: int32 [64, 32, 256], P('gx', 'gy'), may hold values 0 or 1
- stiff_table: float32 [6], replicated, may hold values from 0.3 to 1.2
- perm_table: float32 [6], replicated, may hold values from 0.1 to 0.5
Outputs:
- slab_ends: float32 [8, 5, 64, 32, 256], P('ta', None, 'gx', 'gy')
Inputs may be any that keep to these rules, and one draw needn't show every extreme that they name: `labels`: each label selects one row of the region tables.
All inputs are finite; a program needn't handle non-finite values. No bound on the sum of `ventricle_mask` on one device may be relied on, other than what follows from the above.
Results may differ from a plain program's by a relative error of at most 0.00002.
Values sent between devices are 32-bit elements; how exact they have to be, the bound alone decides.
No kernel may reach another device: no remote copies, remote signals or barrier semaphores. Data moves between devices by JAX's collectives and lax.ppermute only.
A program may use at most 64 MiB of HBM per device.

v0:
```python
import jax
import jax.numpy as jnp
from jax import lax
from jax.sharding import PartitionSpec as P

FINE = 4
ITERS = 2


coupling = 0.3
pressure_gain = 0.4
relax_rate = 0.5
stiffening = 2.0
porosity_ref = 0.2
fine_dt = 0.03


def with_halo(value, sides, width):
    for axis, dim in sides:
        count, length = (lax.axis_size(axis), value.shape[dim])
        up = [(i, (i + 1) % count) for i in range(count - 1)]
        down = [(j, i) for i, j in up]
        last = lax.slice_in_dim(value, length - width, length, axis=dim)
        first = lax.slice_in_dim(value, 0, width, axis=dim)
        before = lax.ppermute(last, axis, up)
        after = lax.ppermute(first, axis, down)
        value = jnp.concatenate([before, value, after], axis=dim)
    return value


def shifted(value, axis, by):
    count = lax.axis_size(axis)
    pairs = [(i, i + by) for i in range(count) if 0 <= i + by < count]
    return lax.ppermute(value, axis, pairs)


def lookup(labels, table):
    onehot = labels[None] == jnp.arange(table.shape[0], dtype=jnp.int32)[:, None, None, None]
    return jnp.sum(
        jnp.where(onehot, table[:, None, None, None], jnp.zeros((), table.dtype)), axis=0
    )


def statics(labels, ventricle_mask, stiff_table, perm_table):
    stiffness = lookup(labels, stiff_table)
    permbase = lookup(labels, perm_table)
    open_cells = 1.0 - ventricle_mask.astype(stiffness.dtype)
    inside = jnp.ones_like(stiffness)
    return jnp.stack([stiffness, permbase, open_cells, inside])


def advance(fields, coeffs, time_step):
    centre = fields[:, 1:-1, 1:-1]
    padded = jnp.pad(centre, ((0, 0), (0, 0), (0, 0), (1, 1)))
    upper = padded[..., 2:]
    lower = padded[..., :-2]
    east = fields[:, 2:, 1:-1]
    west = fields[:, :-2, 1:-1]
    north = fields[:, 1:-1, 2:]
    south = fields[:, 1:-1, :-2]
    stiffness = coeffs[0, 1:-1, 1:-1]
    open_cells = coeffs[2, 1:-1, 1:-1]
    inside = coeffs[3, 1:-1, 1:-1]
    conduct = coeffs[1] * jnp.exp(stiffening * (fields[4] - porosity_ref))
    conduct_mid = conduct[1:-1, 1:-1]
    conduct_pad = jnp.pad(conduct_mid, ((0, 0), (0, 0), (1, 1)))
    press_mid = centre[3]
    flux_sum = 0.5 * (conduct[2:, 1:-1] + conduct_mid) * (east[3] - press_mid)
    flux_sum = flux_sum + 0.5 * (conduct[:-2, 1:-1] + conduct_mid) * (west[3] - press_mid)
    flux_sum = flux_sum + 0.5 * (conduct[1:-1, 2:] + conduct_mid) * (north[3] - press_mid)
    flux_sum = flux_sum + 0.5 * (conduct[1:-1, :-2] + conduct_mid) * (south[3] - press_mid)
    flux_sum = flux_sum + 0.5 * (conduct_pad[:, :, 2:] + conduct_mid) * (upper[3] - press_mid)
    flux_sum = flux_sum + 0.5 * (conduct_pad[:, :, :-2] + conduct_mid) * (lower[3] - press_mid)
    displace_lap = (
        east[0:3]
        + west[0:3]
        + north[0:3]
        + south[0:3]
        + upper[0:3]
        + lower[0:3]
        - 6.0 * centre[0:3]
    )
    press_grad = 0.5 * jnp.stack([east[3] - west[3], north[3] - south[3], upper[3] - lower[3]])
    dilation = 0.5 * (east[0] - west[0] + (north[1] - south[1]) + (upper[2] - lower[2]))
    displace_new = inside * (
        centre[0:3] + time_step * (stiffness * displace_lap - coupling * press_grad)
    )
    press_new = (
        inside
        * open_cells
        * (press_mid + time_step * (flux_sum - pressure_gain * relax_rate * dilation))
    )
    poro_new = inside * (centre[4] + time_step * relax_rate * (1.0 - centre[4]) * dilation)
    return jnp.concatenate([displace_new, press_new[None], poro_new[None]])


def shards(displacement, pressure, porosity, labels, ventricle_mask, stiff_table, perm_table):
    initial = jnp.concatenate([displacement, pressure[None], porosity[None]])
    coeffs = statics(labels, ventricle_mask, stiff_table, perm_table)
    slab_count = lax.axis_size("ta")
    slab_index = lax.axis_index("ta")
    is_first = slab_index == 0
    coeff_one = with_halo(coeffs, (("gx", 1), ("gy", 2)), 1)

    def with_rim(fields):
        return with_halo(fields, (("gx", 1), ("gy", 2)), 1)

    def coarse(fields):
        return advance(with_rim(fields), coeff_one, fine_dt * FINE)

    def fine(fields):
        for _ in range(FINE):
            fields = advance(with_rim(fields), coeff_one, fine_dt)
        return fields

    def sweep(correction):
        begin_state = initial
        for _ in range(slab_count - 1):
            handed = coarse(begin_state)
            if correction is not None:
                handed = handed + correction
            received = shifted(handed, "ta", 1)
            begin_state = jnp.where(is_first, initial, received)
        coarse_out = coarse(begin_state)
        if correction is None:
            end_state = coarse_out
        else:
            end_state = coarse_out + correction
        return (begin_state, coarse_out, end_state)

    begin_state, coarse_old, end_state = sweep(None)
    for _ in range(ITERS):
        correction = fine(begin_state) - coarse_old
        begin_state, coarse_old, end_state = sweep(correction)
    return end_state[None]


def solution(mesh):
    placed = (
        P(None, "gx", "gy", None),
        P("gx", "gy", None),
        P("gx", "gy", None),
        P("gx", "gy", None),
        P("gx", "gy", None),
        P(),
        P(),
    )
    return jax.shard_map(
        shards,
        mesh=mesh,
        in_specs=placed,
        out_specs=P("ta", None, "gx", "gy", None),
        check_vma=False,
    )
```

profile of v0, /device:TPU:6, one launch (start us, length us, event | category | flops | bytes accessed | tf_op | source)
XLA Modules:
  0.0 781.3 jit_solution(9694409868536519648)
XLA Ops:
  8.3 7.5 collective-permute-start.1
  36.0 6.2 collective-permute-done.8
  42.3 6.4 collective-permute-start.10
  50.6 7.6 collective-permute-done.9
  68.8 6.2 collective-permute-done.13
  81.0 5.8 collective-permute-done.14
  97.8 6.2 collective-permute-done.18
  110.0 5.8 collective-permute-done.19
  126.7 6.2 collective-permute-done.23
  138.9 5.8 collective-permute-done.24
  156.4 6.2 collective-permute-done.28
  168.6 5.8 collective-permute-done.29
  186.5 6.2 collective-permute-done.33
  198.7 5.8 collective-permute-done.34
  216.7 6.2 collective-permute-done.38
  228.9 5.8 collective-permute-done.39
  305.3 6.2 collective-permute-done.55
  317.5 5.8 collective-permute-done.56
  335.5 6.2 collective-permute-done.60
  365.7 6.2 collective-permute-done.65
  377.9 5.8 collective-permute-done.66
  395.9 6.2 collective-permute-done.70
  426.1 6.2 collective-permute-done.75
  456.2 6.2 collective-permute-done.80
  486.4 6.2 collective-permute-done.85
  575.1 6.2 collective-permute-done.102
  605.2 6.2 collective-permute-done.107
  635.4 6.2 collective-permute-done.112
  665.5 6.2 collective-permute-done.117
  695.7 6.2 collective-permute-done.122
  725.8 6.2 collective-permute-done.127
  756.0 6.2 collective-permute-done.132
  (560 shorter events, 579.2 us)
Async XLA Ops:
  1.1 16.7 %collective-permute-start.4 = (f32[4,1,8,256]{3,2,1,0:T(8,128)S(1)}, f32[4,1,8,256]{3,2,1,0:T(8,128)S(1)}, u32[]{:S(2)}, u32[]{:S(2)}) collective-permute-start(f32[4,1,8,256]{3,2,1,0:T(8,128)S(1)} %get-tuple-element.354), channel_id=1, source_target_pairs={{0,32},{32,64},{64,96},{96,128},{128,160},{160,192},{192,224},{1,3... | collective-permute-start | bytes 98312 | tf_op jit(solution)/shard_map/ppermute | solution.py:25
  6.3 11.6 %collective-permute-start.5 = (f32[4,1,8,256]{3,2,1,0:T(8,128)S(1)}, f32[4,1,8,256]{3,2,1,0:T(8,128)S(1)}, u32[]{:S(2)}, u32[]{:S(2)}) collective-permute-start(f32[4,1,8,256]{3,2,1,0:T(8,128)S(1)} %get-tuple-element.355), channel_id=1, source_target_pairs={{32,0},{64,32},{96,64},{128,96},{160,128},{192,160},{224,192},{33,... | collective-permute-start | bytes 98312 | tf_op jit(solution)/shard_map/ppermute | solution.py:26
  8.3 12.3 %collective-permute-start.1 = (f32[5,1,8,256]{3,2,1,0:T(8,128)S(1)}, f32[5,1,8,256]{3,2,1,0:T(8,128)S(1)}, u32[]{:S(2)}, u32[]{:S(2)}) collective-permute-start(f32[5,1,8,256]{3,2,1,0:T(8,128)S(1)} %get-tuple-element.352), channel_id=1, source_target_pairs={{0,32},{32,64},{64,96},{96,128},{128,160},{160,192},{192,224},{1,3... | collective-permute-start | bytes 122888 | tf_op jit(solution)/shard_map/ppermute | solution.py:25
  15.8 9.5 %collective-permute-start = (f32[5,1,8,256]{3,2,1,0:T(8,128)S(1)}, f32[5,1,8,256]{3,2,1,0:T(8,128)S(1)}, u32[]{:S(2)}, u32[]{:S(2)}) collective-permute-start(f32[5,1,8,256]{3,2,1,0:T(8,128)S(1)} %get-tuple-element.353), channel_id=1, source_target_pairs={{32,0},{64,32},{96,64},{128,96},{160,128},{192,160},{224,192},{33,... | collective-permute-start | bytes 122888 | tf_op jit(solution)/shard_map/ppermute | solution.py:26
  18.0 10.2 %collective-permute-start.6 = (f32[4,10,1,256]{3,2,1,0:T(1,128)S(1)}, f32[4,10,1,256]{3,2,1,0:T(1,128)S(1)}, u32[]{:S(2)}, u32[]{:S(2)}) collective-permute-start(f32[4,10,1,256]{3,2,1,0:T(1,128)S(1)} %get-tuple-element.350), channel_id=1, source_target_pairs={{0,8},{8,16},{16,24},{1,9},{9,17},{17,25},{2,10},{10,18},{18,26},{... | collective-permute-start | bytes 122888 | tf_op jit(solution)/shard_map/ppermute | solution.py:25
  32.2 10.1 %collective-permute-start.8 = (f32[5,8,8,256]{3,2,1,0:T(8,128)S(1)}, f32[5,8,8,256]{3,2,1,0:T(8,128)S(1)}, u32[]{:S(2)}, u32[]{:S(2)}) collective-permute-start(f32[5,8,8,256]{3,2,1,0:T(8,128)S(1)} %pad_maximum_fusion.8), channel_id=1, source_target_pairs={{0,1},{1,2},{2,3},{3,4},{4,5},{5,6},{6,7},{8,9},{9,10},{10,11},{11... | collective-permute-start | bytes 983048 | tf_op jit(solution)/shard_map/ppermute | solution.py:34
  64.5 10.6 %collective-permute-start.13 = (f32[5,8,8,256]{3,2,1,0:T(8,128)S(1)}, f32[5,8,8,256]{3,2,1,0:T(8,128)S(1)}, u32[]{:S(2)}, u32[]{:S(2)}) collective-permute-start(f32[5,8,8,256]{3,2,1,0:T(8,128)S(1)} %pad_maximum_fusion.9), channel_id=1, source_target_pairs={{0,1},{1,2},{2,3},{3,4},{4,5},{5,6},{6,7},{8,9},{9,10},{10,11},{11... | collective-permute-start | bytes 983048 | tf_op jit(solution)/shard_map/ppermute | solution.py:34
  93.3 10.6 %collective-permute-start.18 = (f32[5,8,8,256]{3,2,1,0:T(8,128)S(1)}, f32[5,8,8,256]{3,2,1,0:T(8,128)S(1)}, u32[]{:S(2)}, u32[]{:S(2)}) collective-permute-start(f32[5,8,8,256]{3,2,1,0:T(8,128)S(1)} %pad_maximum_fusion.10), channel_id=1, source_target_pairs={{0,1},{1,2},{2,3},{3,4},{4,5},{5,6},{6,7},{8,9},{9,10},{10,11},{11... | collective-permute-start | bytes 983048 | tf_op jit(solution)/shard_map/ppermute | solution.py:34
  122.3 10.6 %collective-permute-start.23 = (f32[5,8,8,256]{3,2,1,0:T(8,128)S(1)}, f32[5,8,8,256]{3,2,1,0:T(8,128)S(1)}, u32[]{:S(2)}, u32[]{:S(2)}) collective-permute-start(f32[5,8,8,256]{3,2,1,0:T(8,128)S(1)} %pad_maximum_fusion.11), channel_id=1, source_target_pairs={{0,1},{1,2},{2,3},{3,4},{4,5},{5,6},{6,7},{8,9},{9,10},{10,11},{11... | collective-permute-start | bytes 983048 | tf_op jit(solution)/shard_map/ppermute | solution.py:34
  151.2 11.4 %collective-permute-start.28 = (f32[5,8,8,256]{3,2,1,0:T(8,128)S(1)}, f32[5,8,8,256]{3,2,1,0:T(8,128)S(1)}, u32[]{:S(2)}, u32[]{:S(2)}) collective-permute-start(f32[5,8,8,256]{3,2,1,0:T(8,128)S(1)} %pad_maximum_fusion.12), channel_id=1, source_target_pairs={{0,1},{1,2},{2,3},{3,4},{4,5},{5,6},{6,7},{8,9},{9,10},{10,11},{11... | collective-permute-start | bytes 983048 | tf_op jit(solution)/shard_map/ppermute | solution.py:34
  180.9 11.9 %collective-permute-start.33 = (f32[5,8,8,256]{3,2,1,0:T(8,128)S(1)}, f32[5,8,8,256]{3,2,1,0:T(8,128)S(1)}, u32[]{:S(2)}, u32[]{:S(2)}) collective-permute-start(f32[5,8,8,256]{3,2,1,0:T(8,128)S(1)} %pad_maximum_fusion.13), channel_id=1, source_target_pairs={{0,1},{1,2},{2,3},{3,4},{4,5},{5,6},{6,7},{8,9},{9,10},{10,11},{11... | collective-permute-start | bytes 983048 | tf_op jit(solution)/shard_map/ppermute | solution.py:34
  195.1 9.5 %collective-permute-start.34 = (f32[5,1,8,256]{3,2,1,0:T(8,128)S(1)}, f32[5,1,8,256]{3,2,1,0:T(8,128)S(1)}, u32[]{:S(2)}, u32[]{:S(2)}) collective-permute-start(f32[5,1,8,256]{3,2,1,0:T(8,128)S(1)} %get-tuple-element.332), channel_id=1, source_target_pairs={{32,0},{64,32},{96,64},{128,96},{160,128},{192,160},{224,192},{33,... | collective-permute-start | bytes 122888 | tf_op jit(solution)/shard_map/ppermute | solution.py:26
  211.1 11.9 %collective-permute-start.38 = (f32[5,8,8,256]{3,2,1,0:T(8,128)S(1)}, f32[5,8,8,256]{3,2,1,0:T(8,128)S(1)}, u32[]{:S(2)}, u32[]{:S(2)}) collective-permute-start(f32[5,8,8,256]{3,2,1,0:T(8,128)S(1)} %pad_maximum_fusion.14), channel_id=1, source_target_pairs={{0,1},{1,2},{2,3},{3,4},{4,5},{5,6},{6,7},{8,9},{9,10},{10,11},{11... | collective-permute-start | bytes 983048 | tf_op jit(solution)/shard_map/ppermute | solution.py:34
  225.2 9.5 %collective-permute-start.39 = (f32[5,1,8,256]{3,2,1,0:T(8,128)S(1)}, f32[5,1,8,256]{3,2,1,0:T(8,128)S(1)}, u32[]{:S(2)}, u32[]{:S(2)}) collective-permute-start(f32[5,1,8,256]{3,2,1,0:T(8,128)S(1)} %get-tuple-element.329), channel_id=1, source_target_pairs={{32,0},{64,32},{96,64},{128,96},{160,128},{192,160},{224,192},{33,... | collective-permute-start | bytes 122888 | tf_op jit(solution)/shard_map/ppermute | solution.py:26
  243.5 9.5 %collective-permute-start.43 = (f32[5,1,8,256]{3,2,1,0:T(8,128)S(1)}, f32[5,1,8,256]{3,2,1,0:T(8,128)S(1)}, u32[]{:S(2)}, u32[]{:S(2)}) collective-permute-start(f32[5,1,8,256]{3,2,1,0:T(8,128)S(1)} %get-tuple-element.325), channel_id=1, source_target_pairs={{32,0},{64,32},{96,64},{128,96},{160,128},{192,160},{224,192},{33,... | collective-permute-start | bytes 122888 | tf_op jit(solution)/shard_map/ppermute | solution.py:26
  263.0 9.5 %collective-permute-start.47 = (f32[5,1,8,256]{3,2,1,0:T(8,128)S(1)}, f32[5,1,8,256]{3,2,1,0:T(8,128)S(1)}, u32[]{:S(2)}, u32[]{:S(2)}) collective-permute-start(f32[5,1,8,256]{3,2,1,0:T(8,128)S(1)} %get-tuple-element.321), channel_id=1, source_target_pairs={{32,0},{64,32},{96,64},{128,96},{160,128},{192,160},{224,192},{33,... | collective-permute-start | bytes 122888 | tf_op jit(solution)/shard_map/ppermute | solution.py:26
  299.7 11.9 %collective-permute-start.55 = (f32[5,8,8,256]{3,2,1,0:T(8,128)S(1)}, f32[5,8,8,256]{3,2,1,0:T(8,128)S(1)}, u32[]{:S(2)}, u32[]{:S(2)}) collective-permute-start(f32[5,8,8,256]{3,2,1,0:T(8,128)S(1)} %get-tuple-element.105), channel_id=1, source_target_pairs={{0,1},{1,2},{2,3},{3,4},{4,5},{5,6},{6,7},{8,9},{9,10},{10,11},{11... | collective-permute-start | bytes 983048 | tf_op jit(solution)/shard_map/ppermute | solution.py:34
  313.8 9.5 %collective-permute-start.56 = (f32[5,1,8,256]{3,2,1,0:T(8,128)S(1)}, f32[5,1,8,256]{3,2,1,0:T(8,128)S(1)}, u32[]{:S(2)}, u32[]{:S(2)}) collective-permute-start(f32[5,1,8,256]{3,2,1,0:T(8,128)S(1)} %get-tuple-element.313), channel_id=1, source_target_pairs={{32,0},{64,32},{96,64},{128,96},{160,128},{192,160},{224,192},{33,... | collective-permute-start | bytes 122888 | tf_op jit(solution)/shard_map/ppermute | solution.py:26
  329.9 11.9 %collective-permute-start.60 = (f32[5,8,8,256]{3,2,1,0:T(8,128)S(1)}, f32[5,8,8,256]{3,2,1,0:T(8,128)S(1)}, u32[]{:S(2)}, u32[]{:S(2)}) collective-permute-start(f32[5,8,8,256]{3,2,1,0:T(8,128)S(1)} %maximum_add_fusion), channel_id=1, source_target_pairs={{0,1},{1,2},{2,3},{3,4},{4,5},{5,6},{6,7},{8,9},{9,10},{10,11},{11... | collective-permute-start | bytes 983048 | tf_op jit(solution)/shard_map/ppermute | solution.py:34
  360.1 11.9 %collective-permute-start.65 = (f32[5,8,8,256]{3,2,1,0:T(8,128)S(1)}, f32[5,8,8,256]{3,2,1,0:T(8,128)S(1)}, u32[]{:S(2)}, u32[]{:S(2)}) collective-permute-start(f32[5,8,8,256]{3,2,1,0:T(8,128)S(1)} %maximum_add_fusion.1), channel_id=1, source_target_pairs={{0,1},{1,2},{2,3},{3,4},{4,5},{5,6},{6,7},{8,9},{9,10},{10,11},{11... | collective-permute-start | bytes 983048 | tf_op jit(solution)/shard_map/ppermute | solution.py:34
  374.2 9.5 %collective-permute-start.66 = (f32[5,1,8,256]{3,2,1,0:T(8,128)S(1)}, f32[5,1,8,256]{3,2,1,0:T(8,128)S(1)}, u32[]{:S(2)}, u32[]{:S(2)}) collective-permute-start(f32[5,1,8,256]{3,2,1,0:T(8,128)S(1)} %get-tuple-element.307), channel_id=1, source_target_pairs={{32,0},{64,32},{96,64},{128,96},{160,128},{192,160},{224,192},{33,... | collective-permute-start | bytes 122888 | tf_op jit(solution)/shard_map/ppermute | solution.py:26
  390.3 11.9 %collective-permute-start.70 = (f32[5,8,8,256]{3,2,1,0:T(8,128)S(1)}, f32[5,8,8,256]{3,2,1,0:T(8,128)S(1)}, u32[]{:S(2)}, u32[]{:S(2)}) collective-permute-start(f32[5,8,8,256]{3,2,1,0:T(8,128)S(1)} %maximum_add_fusion.2), channel_id=1, source_target_pairs={{0,1},{1,2},{2,3},{3,4},{4,5},{5,6},{6,7},{8,9},{9,10},{10,11},{11... | collective-permute-start | bytes 983048 | tf_op jit(solution)/shard_map/ppermute | solution.py:34
  420.4 11.9 %collective-permute-start.75 = (f32[5,8,8,256]{3,2,1,0:T(8,128)S(1)}, f32[5,8,8,256]{3,2,1,0:T(8,128)S(1)}, u32[]{:S(2)}, u32[]{:S(2)}) collective-permute-start(f32[5,8,8,256]{3,2,1,0:T(8,128)S(1)} %maximum_add_fusion.3), channel_id=1, source_target_pairs={{0,1},{1,2},{2,3},{3,4},{4,5},{5,6},{6,7},{8,9},{9,10},{10,11},{11... | collective-permute-start | bytes 983048 | tf_op jit(solution)/shard_map/ppermute | solution.py:34
  450.6 11.9 %collective-permute-start.80 = (f32[5,8,8,256]{3,2,1,0:T(8,128)S(1)}, f32[5,8,8,256]{3,2,1,0:T(8,128)S(1)}, u32[]{:S(2)}, u32[]{:S(2)}) collective-permute-start(f32[5,8,8,256]{3,2,1,0:T(8,128)S(1)} %maximum_add_fusion.4), channel_id=1, source_target_pairs={{0,1},{1,2},{2,3},{3,4},{4,5},{5,6},{6,7},{8,9},{9,10},{10,11},{11... | collective-permute-start | bytes 983048 | tf_op jit(solution)/shard_map/ppermute | solution.py:34
  480.8 11.9 %collective-permute-start.85 = (f32[5,8,8,256]{3,2,1,0:T(8,128)S(1)}, f32[5,8,8,256]{3,2,1,0:T(8,128)S(1)}, u32[]{:S(2)}, u32[]{:S(2)}) collective-permute-start(f32[5,8,8,256]{3,2,1,0:T(8,128)S(1)} %maximum_add_fusion.5), channel_id=1, source_target_pairs={{0,1},{1,2},{2,3},{3,4},{4,5},{5,6},{6,7},{8,9},{9,10},{10,11},{11... | collective-permute-start | bytes 983048 | tf_op jit(solution)/shard_map/ppermute | solution.py:34
  569.4 11.9 %collective-permute-start.102 = (f32[5,8,8,256]{3,2,1,0:T(8,128)S(1)}, f32[5,8,8,256]{3,2,1,0:T(8,128)S(1)}, u32[]{:S(2)}, u32[]{:S(2)}) collective-permute-start(f32[5,8,8,256]{3,2,1,0:T(8,128)S(1)} %get-tuple-element.47), channel_id=1, source_target_pairs={{0,1},{1,2},{2,3},{3,4},{4,5},{5,6},{6,7},{8,9},{9,10},{10,11},{11... | collective-permute-start | bytes 983048 | tf_op jit(solution)/shard_map/ppermute | solution.py:34
  599.6 11.9 %collective-permute-start.107 = (f32[5,8,8,256]{3,2,1,0:T(8,128)S(1)}, f32[5,8,8,256]{3,2,1,0:T(8,128)S(1)}, u32[]{:S(2)}, u32[]{:S(2)}) collective-permute-start(f32[5,8,8,256]{3,2,1,0:T(8,128)S(1)} %maximum_add_fusion.6), channel_id=1, source_target_pairs={{0,1},{1,2},{2,3},{3,4},{4,5},{5,6},{6,7},{8,9},{9,10},{10,11},{11... | collective-permute-start | bytes 983048 | tf_op jit(solution)/shard_map/ppermute | solution.py:34
  629.7 11.9 %collective-permute-start.112 = (f32[5,8,8,256]{3,2,1,0:T(8,128)S(1)}, f32[5,8,8,256]{3,2,1,0:T(8,128)S(1)}, u32[]{:S(2)}, u32[]{:S(2)}) collective-permute-start(f32[5,8,8,256]{3,2,1,0:T(8,128)S(1)} %maximum_add_fusion.7), channel_id=1, source_target_pairs={{0,1},{1,2},{2,3},{3,4},{4,5},{5,6},{6,7},{8,9},{9,10},{10,11},{11... | collective-permute-start | bytes 983048 | tf_op jit(solution)/shard_map/ppermute | solution.py:34
  659.9 11.9 %collective-permute-start.117 = (f32[5,8,8,256]{3,2,1,0:T(8,128)S(1)}, f32[5,8,8,256]{3,2,1,0:T(8,128)S(1)}, u32[]{:S(2)}, u32[]{:S(2)}) collective-permute-start(f32[5,8,8,256]{3,2,1,0:T(8,128)S(1)} %maximum_add_fusion.8), channel_id=1, source_target_pairs={{0,1},{1,2},{2,3},{3,4},{4,5},{5,6},{6,7},{8,9},{9,10},{10,11},{11... | collective-permute-start | bytes 983048 | tf_op jit(solution)/shard_map/ppermute | solution.py:34
  690.1 11.9 %collective-permute-start.122 = (f32[5,8,8,256]{3,2,1,0:T(8,128)S(1)}, f32[5,8,8,256]{3,2,1,0:T(8,128)S(1)}, u32[]{:S(2)}, u32[]{:S(2)}) collective-permute-start(f32[5,8,8,256]{3,2,1,0:T(8,128)S(1)} %maximum_add_fusion.9), channel_id=1, source_target_pairs={{0,1},{1,2},{2,3},{3,4},{4,5},{5,6},{6,7},{8,9},{9,10},{10,11},{11... | collective-permute-start | bytes 983048 | tf_op jit(solution)/shard_map/ppermute | solution.py:34
  720.2 11.9 %collective-permute-start.127 = (f32[5,8,8,256]{3,2,1,0:T(8,128)S(1)}, f32[5,8,8,256]{3,2,1,0:T(8,128)S(1)}, u32[]{:S(2)}, u32[]{:S(2)}) collective-permute-start(f32[5,8,8,256]{3,2,1,0:T(8,128)S(1)} %maximum_add_fusion.10), channel_id=1, source_target_pairs={{0,1},{1,2},{2,3},{3,4},{4,5},{5,6},{6,7},{8,9},{9,10},{10,11},{11... | collective-permute-start | bytes 983048 | tf_op jit(solution)/shard_map/ppermute | solution.py:34
  750.4 11.9 %collective-permute-start.132 = (f32[5,8,8,256]{3,2,1,0:T(8,128)S(1)}, f32[5,8,8,256]{3,2,1,0:T(8,128)S(1)}, u32[]{:S(2)}, u32[]{:S(2)}) collective-permute-start(f32[5,8,8,256]{3,2,1,0:T(8,128)S(1)} %maximum_add_fusion.11), channel_id=1, source_target_pairs={{0,1},{1,2},{2,3},{3,4},{4,5},{5,6},{6,7},{8,9},{9,10},{10,11},{11... | collective-permute-start | bytes 983048 | tf_op jit(solution)/shard_map/ppermute | solution.py:34
  (112 other events, 601.9 us)
where the time goes:
time: 794 us; the launch traced here: 781 us
  starting transfers between devices  400 us (50%)
  waiting for transfers between devices  354 us (45%)
  other arithmetic  22.9 us (3%)
    ppermute x58, waiting for transfers between devices, with_halo(): after = lax.ppermute(first, axis, down)  223 us
    ppermute x58, starting transfers between devices, with_halo(): before = lax.ppermute(last, axis, up)  150 us
    ppermute x58, starting transfers between devices, with_halo(): after = lax.ppermute(first, axis, down)  138 us
    ppermute x21, waiting for transfers between devices, shifted(): return lax.ppermute(value, axis, pairs)  131 us
    ppermute x21, starting transfers between devices, shifted(): return lax.ppermute(value, axis, pairs)  112 us
  transfers between devices with their start and end apart: 137, of which 77 were waited for; matrix products, arithmetic and copies ran while one was open for 0% of the time, Pallas kernels for 0%

commit v1 on v0

v1 whole, which is shorter than its diff:
```python
import math

import jax
import jax.numpy as jnp
from jax import lax
from jax.experimental import pallas as pl
from jax.experimental.pallas import tpu as pltpu
from jax.sharding import PartitionSpec as P

FINE = 4
coupling = 0.3
pressure_gain = 0.4
relax_rate = 0.5
stiffening = 2.0
porosity_ref = 0.2
fine_dt = 0.03

F32 = jnp.float32
INTERPRET = False

DEPTH = 15
CHUNK = 104
PLANE = 32
FIELD = 16 * PLANE
SLOT = 6 * FIELD
A0, B0, T0, SLOTS = 0, 8, 17, 19
LAST = DEPTH - 1


def lanes():
    return lax.broadcasted_iota(jnp.int32, (8, 128), 1)


def exchange_bits(v):
    lane = lanes()
    for b in range(3):
        high = ((lane >> (3 + b)) & 1) == 1
        step = 8 << b
        new = list(v)
        for i in range(8):
            if not (i >> b) & 1:
                j = i | (1 << b)
                new[i] = jnp.where(high, pltpu.roll(v[j], step, 1), v[i])
                new[j] = jnp.where(high, v[j], pltpu.roll(v[i], 128 - step, 1))
        v = new
    return v


def pack_kernel(ta_ref, disp, pres, poro, lab, mask, out, flat, big, win, rev):
    ta = ta_ref[0]
    for f in range(7):
        field = disp[f] if f < 3 else (pres, poro, lab, mask)[f - 3][...].astype(F32)
        for h in range(2):
            flat[(f * 2 + h) * 64 : (f * 2 + h + 1) * 64, :] = field[:, h * 128 : (h + 1) * 128]

    def rows(f, h):
        return [flat[pl.ds((f * 2 + h) * 64 + y, 8, stride=8), :] for y in range(8)]

    big[:, 0:16, :] = jnp.zeros((4, 16, 128), F32)
    big[:, 272:288, :] = jnp.zeros((4, 16, 128), F32)
    for t in range(4):
        for h in range(2):
            pair = jnp.concatenate(rows(2 * t, h) + rows(min(2 * t + 1, 6), h), axis=0)
            big[t, 16 + h * 128 : 144 + h * 128, :] = pair.T
        win[t, :, :] = big[t, pl.ds(pl.multiple_of(ta * 32, 32), 64), :]
        for i in range(64):
            rev[t, i : i + 1, :] = win[t, 63 - i : 64 - i, :]
        win[t + 4, :, :] = pltpu.roll(win[t, :, :], 64, 1)
        rev[t + 4, :, :] = pltpu.roll(rev[t, :, :], 64, 1)
    low = lax.broadcasted_iota(jnp.int32, (15, 128), 1) < 64
    for g in range(32):
        for f in range(7):
            t = f // 2
            first = win[t + 4 * (f % 2), g + 2 : g + 17, :]
            second = rev[t + 4 * (1 - f % 2), 32 - g : 47 - g, :]
            both = jnp.where(low, first, second)
            if f < 5:
                out[g * CHUNK + f * 15 : g * CHUNK + f * 15 + 15, :] = both
            else:
                at = g * CHUNK + 75 + (f - 5) * 14
                out[at : at + 14, :] = both[1:, :]
        out[g * CHUNK + 103 : g * CHUNK + 104, :] = jnp.zeros((1, 128), F32)


def main_kernel(c_ref, stiff_tab, perm_tab, recv, out, st, raw, co, inside, ends):
    lane = lanes()
    row = lax.broadcasted_iota(jnp.int32, (8, 128), 0)
    half0 = lane < 64
    x = lane & 63
    has_e, has_w = x < 63, x > 0
    has_n, has_s = row < 7, row > 0
    zero = jnp.zeros((8, 128), F32)

    def tile(start):
        return pl.ds(pl.multiple_of(start, 8), 8)

    def base(slot, f, zl):
        return slot * SLOT + f * FIELD + zl * PLANE

    def relayout(group, carry):
        for gy in range(4):
            v = [recv[tile((gx * 4 + gy) * CHUNK + group * 8), :] for gx in range(8)]
            v = exchange_bits(v)
            for yq in range(8):
                place = (yq % 4) * 8 + 2 * gy + yq // 4
                raw[pl.ds(group * (8 * PLANE) + place, 8, stride=PLANE), :] = v[yq]
        return carry

    lax.fori_loop(0, CHUNK // 8, relayout, 0)

    c = c_ref[0]
    scale = stiffening * math.log2(math.e)

    def conduct(perm, phi):
        return perm * jnp.exp2((phi - porosity_ref) * scale)

    def coefficients(zl, carry):
        z = jnp.where(half0, c - 14 + zl, c + 15 - zl)
        m = jnp.where((z >= 0) & (z < 256), 1.0, 0.0).astype(F32)
        inside[tile(zl * 8), :] = m
        for yl in range(4):
            label = raw[tile((74 + zl) * PLANE + 8 * yl), :]
            drain = raw[tile((88 + zl) * PLANE + 8 * yl), :]
            stiff, perm = zero, zero
            for i in range(6):
                hit = label == float(i)
                stiff = jnp.where(hit, stiff_tab[i], stiff)
                perm = jnp.where(hit, perm_tab[i], perm)
            stiff = stiff * m
            fine_a = stiff * fine_dt
            coarse_a = stiff * (fine_dt * FINE)
            values = (
                fine_a,
                1.0 - 6.0 * fine_a,
                coarse_a,
                1.0 - 6.0 * coarse_a,
                (1.0 - drain) * m,
                perm * m * (0.5 * fine_dt),
            )
            for i, value in enumerate(values):
                co[tile((i * DEPTH + zl) * PLANE + 8 * yl), :] = value
        return carry

    lax.fori_loop(1, DEPTH, coefficients, 0)
    for yl in range(4):
        co[tile(5 * DEPTH * PLANE + 8 * yl), :] = zero

    sign = jnp.where(half0, 1.0, -1.0).astype(F32)

    def put(slot, zl, yl, vals, k=None, last=False):
        for f in range(5):
            st[tile(base(slot, f, zl) + 8 * yl), :] = vals[f]
        if k is not None:
            st[tile(base(slot, 5, zl) + 8 * yl), :] = k
            if last:
                for f, v in ((0, vals[0]), (1, vals[1]), (2, -vals[2]), (3, vals[3]), (5, k)):
                    st[tile(base(slot, f, DEPTH) + 8 * yl), :] = pltpu.roll(v, 64, 1)

    def get(slot, f, zl, yl):
        return st[tile(base(slot, f, zl) + 8 * yl), :]

    def coef(i, zl, yl):
        return co[tile((i * DEPTH + zl) * PLANE + 8 * yl), :]

    def sweep(first, body):
        def step(zl, carry):
            body(zl, False)
            return carry

        lax.fori_loop(first, LAST, step, 0)
        body(LAST, True)

    def stage_start(zl, last):
        for yl in range(4):
            vals = [raw[tile((f * 15 + zl) * PLANE + 8 * yl), :] for f in range(5)]
            vals[2] = vals[2] * sign
            put(A0, zl, yl, vals, conduct(coef(5, zl, yl), vals[4]), last)

    sweep(0, stage_start)

    def advance(src, zl, fine, emit):
        dt = fine_dt if fine else fine_dt * FINE
        at = base(src, 0, zl)

        def load(f, yl, dz=0):
            return st[tile(at + f * FIELD + dz * PLANE + 8 * yl), :]

        m = inside[tile(zl * 8), :]
        grad_c = m * (dt * coupling * 0.5)
        poro_c = m * (dt * relax_rate * 0.5)
        cen = {f: [load(f, yl) for yl in range(4)] for f in (0, 1, 2, 3, 5)}
        up = {f: jnp.where(has_n, pltpu.roll(cen[f][0], 7, 0), 0.0) for f in cen}
        dn = {f: jnp.where(has_s, pltpu.roll(cen[f][3], 1, 0), 0.0) for f in cen}
        face = (dn[5] + cen[5][0]) * (cen[3][0] - dn[3])
        for yl in range(4):
            mid = {f: cen[f][yl] for f in cen}
            e = {f: jnp.where(has_e, pltpu.roll(mid[f], 127, 1), 0.0) for f in cen}
            w = {f: jnp.where(has_w, pltpu.roll(mid[f], 1, 1), 0.0) for f in cen}
            n = {f: cen[f][yl + 1] if yl < 3 else up[f] for f in cen}
            s = {f: cen[f][yl - 1] if yl > 0 else dn[f] for f in cen}
            i = {f: load(f, yl, 1) for f in cen}
            o = {f: load(f, yl, -1) for f in cen}
            p, k = mid[3], mid[5]
            next_face = (n[5] + k) * (n[3] - p)
            flux = next_face - face
            face = next_face
            for side in (e, w, i, o):
                flux = flux + (side[5] + k) * (side[3] - p)
            dil = (e[0] - w[0]) + (n[1] - s[1]) + (i[2] - o[2])
            grads = (e[3] - w[3], n[3] - s[3], i[3] - o[3])
            a = coef(0 if fine else 2, zl, yl)
            a6 = coef(1 if fine else 3, zl, yl)
            new = []
            for f in range(3):
                around = (e[f] + w[f]) + (n[f] + s[f]) + (i[f] + o[f])
                new.append(a * around + a6 * mid[f] - grad_c * grads[f])
            if not fine:
                flux = flux * float(FINE)
            gain = dt * pressure_gain * relax_rate * 0.5
            new.append(coef(4, zl, yl) * (p + (flux - gain * dil)))
            phi = load(4, yl)
            new.append(phi + (poro_c * dil) * (1.0 - phi))
            emit(yl, new)

    def plain(src, dst, first, fine):
        def body(zl, last):
            def emit(yl, new):
                put(dst, zl, yl, new, conduct(coef(5, zl, yl), new[4]), last)

            advance(src, zl, fine, emit)

        sweep(first, body)

    def minus(src, sub, dst, first):
        def body(zl, last):
            def emit(yl, new):
                put(dst, zl, yl, [new[f] - get(sub, f, zl, yl) for f in range(5)])

            advance(src, zl, True, emit)

        sweep(first, body)

    def plus(src, cor, dst, first, keep):
        def body(zl, last):
            def emit(yl, new):
                vals = [new[f] + get(cor, f, zl, yl) for f in range(5)]
                if keep:
                    put(cor, zl, yl, new)
                put(dst, zl, yl, vals, conduct(coef(5, zl, yl), vals[4]), last)

            advance(src, zl, False, emit)

        sweep(first, body)

    def fine_all(source, start, count):
        def slab(j, carry):
            def inner(s, carry):
                src = jnp.where(s == 0, source + j, T0 + ((s + 1) & 1))
                plain(src, T0 + (s & 1), start + j + s, True)
                return carry

            lax.fori_loop(0, FINE - 1, inner, 0)
            minus(T0, A0 + j + 1, A0 + j, start + j + FINE - 1)

            @pl.when(j == 0)
            def _():
                for yl in range(4):
                    put(B0, LAST, yl, [get(B0 + 1, f, LAST, yl) for f in range(5)])

                def body(zl, last):
                    for yl in range(4):
                        vals = [get(A0 + 1, f, zl, yl) + get(A0, f, zl, yl) for f in range(5)]
                        put(B0 + 1, zl, yl, vals, conduct(coef(5, zl, yl), vals[4]), last)

                sweep(start + FINE - 1, body)

            return carry

        lax.fori_loop(0, count, slab, 0)

    def chain0(k, carry):
        plain(A0 + k, A0 + k + 1, jnp.where(k == 6, 10, k + 1), False)
        return carry

    lax.fori_loop(0, 7, chain0, 0)
    fine_all(A0, 1, 7)

    def chain1(k, carry):
        plus(B0 + k, A0 + k, B0 + k + 1, jnp.where(k == 7, 14, k + 4), True)
        return carry

    lax.fori_loop(1, 8, chain1, 0)
    fine_all(B0 + 1, 5, 7)

    def chain2(k, carry):
        plus(B0 + k - 1, A0 + k - 1, B0 + k, k + 7, False)
        return carry

    lax.fori_loop(2, 8, chain2, 0)

    for t in range(3):
        for gy in range(4):
            v = []
            for yq in range(8):
                place = (yq % 4) * 8 + 2 * gy + yq // 4
                first = st[pl.ds(B0 * SLOT + 2 * t * FIELD + LAST * PLANE + place, 8, stride=SLOT), :]
                if t < 2:
                    second = st[pl.ds(B0 * SLOT + (2 * t + 1) * FIELD + LAST * PLANE + place, 8, stride=SLOT), :]
                    second = pltpu.roll(second, 64, 1)
                else:
                    second = zero
                v.append(jnp.where(half0, first, second))
            v = exchange_bits(v)
            for gx in range(8):
                ends[pl.ds(t * 256 + gx * 4 + gy, 8, stride=32), :] = v[gx]
        out[:, t * 128 : (t + 1) * 128] = ends[t * 256 : (t + 1) * 256, :]


def unpack_kernel(recv, out, turned):
    for t in range(3):
        for h in range(2):
            block = recv[h * 128 : (h + 1) * 128, t * 128 : (t + 1) * 128]
            turned[h * 384 + t * 128 : h * 384 + (t + 1) * 128, :] = block.T
    for f in range(5):
        for x in range(8):
            for h in range(2):
                at = (f * 8 + x) * 8
                out[at : at + 8, h * 128 : (h + 1) * 128] = turned[pl.ds(h * 384 + f * 64 + x, 8, stride=8), :]


def vmem(n=None):
    return pl.BlockSpec(memory_space=pltpu.VMEM)


def smem():
    return pl.BlockSpec(memory_space=pltpu.SMEM)


def pack(ta, disp, pres, poro, lab, mask):
    return pl.pallas_call(
        pack_kernel,
        out_shape=jax.ShapeDtypeStruct((32 * CHUNK, 128), F32),
        in_specs=[smem()] + [vmem()] * 5,
        out_specs=vmem(),
        scratch_shapes=[
            pltpu.VMEM((7 * 2 * 64, 128), F32),
            pltpu.VMEM((4, 288, 128), F32),
            pltpu.VMEM((8, 64, 128), F32),
            pltpu.VMEM((8, 64, 128), F32),
        ],
        interpret=INTERPRET,
        name="pack",
    )(ta, disp, pres, poro, lab, mask)


def compute(c, stiff_table, perm_table, recv):
    return pl.pallas_call(
        main_kernel,
        out_shape=jax.ShapeDtypeStruct((256, 384), F32),
        in_specs=[smem(), smem(), smem(), vmem()],
        out_specs=vmem(),
        scratch_shapes=[
            pltpu.VMEM((SLOTS * SLOT, 128), F32),
            pltpu.VMEM((CHUNK * PLANE, 128), F32),
            pltpu.VMEM((6 * DEPTH * PLANE, 128), F32),
            pltpu.VMEM((DEPTH * 8, 128), F32),
            pltpu.VMEM((3 * 256, 128), F32),
        ],
        compiler_params=pltpu.CompilerParams(vmem_limit_bytes=48 << 20),
        interpret=INTERPRET,
        name="parareal",
    )(c, stiff_table, perm_table, recv)


def unpack(recv):
    return pl.pallas_call(
        unpack_kernel,
        out_shape=jax.ShapeDtypeStruct((320, 256), F32),
        in_specs=[vmem()],
        out_specs=vmem(),
        scratch_shapes=[pltpu.VMEM((768, 128), F32)],
        interpret=INTERPRET,
        name="unpack",
    )(recv)


def shards(displacement, pressure, porosity, labels, ventricle_mask, stiff_table, perm_table):
    ta = lax.axis_index("ta").astype(jnp.int32)
    plane = ta * 32 + lax.axis_index("gx") * 4 + lax.axis_index("gy")
    flat = lambda a: a.reshape(a.shape[:-3] + (64, 256))
    sent = pack(
        ta.reshape(1), flat(displacement), flat(pressure), flat(porosity), flat(labels), flat(ventricle_mask)
    )
    got = lax.all_to_all(sent.reshape(32, CHUNK, 128), ("gx", "gy"), 0, 0, tiled=True)
    ends = compute(plane.astype(jnp.int32).reshape(1), stiff_table, perm_table, got.reshape(32 * CHUNK, 128))
    mine = lax.all_to_all(ends, ("ta", "gx", "gy"), 0, 0, tiled=True)
    return unpack(mine).reshape(1, 5, 8, 8, 256)


def solution(mesh):
    placed = (
        P(None, "gx", "gy", None),
        P("gx", "gy", None),
        P("gx", "gy", None),
        P("gx", "gy", None),
        P("gx", "gy", None),
        P(),
        P(),
    )
    return jax.shard_map(
        shards,
        mesh=mesh,
        in_specs=placed,
        out_specs=P("ta", None, "gx", "gy", None),
        check_vma=False,
    )
```

time: 794 us -> 164 us (0.21); the launches traced: 781 us -> 162 us
  starting transfers between devices: 400 us -> 7.7 us
  waiting for transfers between devices: 354 us -> 24 us
  Pallas kernels: 0 us -> 101 us
  blocking collectives: 0 us -> 28.6 us
  other arithmetic: 22.9 us -> 0 us
    ppermute x137 -> x0, starting transfers between devices: 400 us -> none  [the longest x58 150 us: with_halo(): before = lax.ppermute(last, axis, up)]
    ppermute x137 -> x0, waiting for transfers between devices: 354 us -> none  [the longest x58 223 us: with_halo(): after = lax.ppermute(first, axis, down)]
    pallas_call x0 -> x3, Pallas kernels: none -> 101 us  [the longest x1 96.4 us: compute(): pl.pallas_call(main_kernel, out_shape=jax.ShapeDtypeStruct((256, 384), F3...]
    all_to_all x0 -> x1, blocking collectives: none -> 28.6 us  [shards(): mine = lax.all_to_all(ends, ('ta', 'gx', 'gy'), 0, 0, tiled=True)]
    all_to_all x0 -> x1, waiting for transfers between devices: none -> 24 us  [shards(): lax.all_to_all(sent.reshape(32, CHUNK, 128), ('gx', 'gy'), 0, 0, tiled=True)]
  transfers between devices with their start and end apart: 137 -> 1, of which waited for: 77 -> 1; matrix products, arithmetic and copies ran while one was open for 0% -> 0% of each run, Pallas kernels for 0% -> 0%
where the time goes in v1:
time: 164 us; the launch traced here: 162 us
  Pallas kernels  101 us (62%)
  blocking collectives  28.6 us (17%)
  waiting for transfers between devices  24 us (15%)
  starting transfers between devices  7.7 us (5%)
    pallas_call x1, Pallas kernels, compute(): pl.pallas_call(main_kernel, out_shape=jax.ShapeDtypeStruct((256, 384), F3...  96.4 us
    all_to_all x1, blocking collectives, shards(): mine = lax.all_to_all(ends, ('ta', 'gx', 'gy'), 0, 0, tiled=True)  28.6 us
    all_to_all x1, waiting for transfers between devices, shards(): lax.all_to_all(sent.reshape(32, CHUNK, 128), ('gx', 'gy'), 0, 0, tiled=True)  24 us
    all_to_all x1, starting transfers between devices, shards(): lax.all_to_all(sent.reshape(32, CHUNK, 128), ('gx', 'gy'), 0, 0, tiled=True)  7.7 us
  transfers between devices with their start and end apart: 1, of which 1 were waited for; matrix products, arithmetic and copies ran while one was open for 0% of the time, Pallas kernels for 0%

profile of v1, /device:TPU:6, one launch (start us, length us, event | category | flops | bytes accessed | tf_op | source)
XLA Modules:
  0.0 162.5 jit_solution(5831152006270281531)
XLA Ops:
  0.0 2.7 %pack.1 = f32[3328,128]{1,0:T(8,128)} custom-call(s32[1]{0:T(128)} %bitcast.1.ta_ref, f32[3,64,256]{2,1,0:T(8,128)} %bitcast.18, f32[64,256]{1,0:T(8,128)} %bitcast.19, f32[64,256]{1,0:T(8,128)} %bitcast.20, s32[64,256]{1,0:T(8,128)} %bitcast.21, s32[64,256]{1,0:T(8,128)} %bitcast.22), custom_call_target="tpu_custom_call" | custom-call | tf_op jit(solution)/shard_map/pack/pallas_call | solution.py:340
  2.7 0.0 copy-start
  2.7 0.0 copy-start.1
  2.7 7.7 %all-to-all-start = ((f32[32,104,128]{2,1,0:T(8,128)}), f32[32,104,128]{2,1,0:T(8,128)S(1)}, u32[]{:S(2)}, u32[]{:S(2)}) async-start(f32[32,104,128]{2,1,0:T(8,128)} %bitcast.16), calls=%async_computation | async-start | bytes 3407872 | tf_op jit(solution)/shard_map/all_to_all | solution.py:394
  10.4 24.0 %all-to-all-done = f32[32,104,128]{2,1,0:T(8,128)S(1)} async-done(((f32[32,104,128]{2,1,0:T(8,128)}), f32[32,104,128]{2,1,0:T(8,128)S(1)}, u32[]{:S(2)}, u32[]{:S(2)}) %all-to-all-start) | async-done | bytes 1703968 | tf_op jit(solution)/shard_map/all_to_all | solution.py:394
  34.4 0.0 copy-done
  34.4 0.0 copy-done.1
  34.4 96.4 %parareal.1 = f32[256,384]{1,0:T(8,128)S(1)} custom-call(s32[1]{0:T(128)} %bitcast.c_ref, f32[6]{0:T(128)S(1)} %copy-done, f32[6]{0:T(128)S(1)} %copy-done.1, f32[3328,128]{1,0:T(8,128)S(1)} %bitcast.14), custom_call_target="tpu_custom_call" | custom-call | tf_op jit(solution)/shard_map/parareal/pallas_call | solution.py:357
  130.8 0.4 copy.8
  131.2 28.6 %all_to_all.16 = f32[256,1,384]{2,1,0:T(1,128)S(1)} all-to-all(f32[256,1,384]{2,1,0:T(1,128)S(1)} %copy.8), channel_id=1, replica_groups=mesh['gx'=8,'gy'=4,'ta'=8] {'ta','gx','gy'}, dimensions={0} | all-to-all | bytes 786432 | tf_op jit(solution)/shard_map/all_to_all | solution.py:396
  159.8 0.8 copy.11
  160.6 1.9 %unpack.1 = f32[320,256]{1,0:T(8,128)} custom-call(f32[256,384]{1,0:T(8,128)} %bitcast.17), custom_call_target="tpu_custom_call" | custom-call | tf_op jit(solution)/shard_map/unpack/pallas_call | solution.py:376
Async XLA Ops:
  2.7 31.7 %copy-start = (f32[6]{0:T(128)S(1)}, f32[6]{0:T(128)}, u32[]{:S(2)}) copy-start(f32[6]{0:T(128)} %stiff_tab.1) | copy-start | bytes 76
  2.7 31.7 %copy-start.1 = (f32[6]{0:T(128)S(1)}, f32[6]{0:T(128)}, u32[]{:S(2)}) copy-start(f32[6]{0:T(128)} %perm_tab.1) | copy-start | bytes 76
  2.7 31.7 %all-to-all-start = ((f32[32,104,128]{2,1,0:T(8,128)}), f32[32,104,128]{2,1,0:T(8,128)S(1)}, u32[]{:S(2)}, u32[]{:S(2)}) async-start(f32[32,104,128]{2,1,0:T(8,128)} %bitcast.16), calls=%async_computation | async-start | bytes 3407872 | tf_op jit(solution)/shard_map/all_to_all | solution.py:394

commit v2 on v0

v2 whole, which is shorter than its diff:
```python
import math

import jax
import jax.numpy as jnp
from jax import lax
from jax.experimental import pallas as pl
from jax.experimental.pallas import tpu as pltpu
from jax.sharding import PartitionSpec as P

FINE = 4
coupling = 0.3
pressure_gain = 0.4
relax_rate = 0.5
stiffening = 2.0
porosity_ref = 0.2
fine_dt = 0.03

F32 = jnp.float32
INTERPRET = False

REACH = 18
ROWS = 128
PLANE = 24
FIELD = 19 * PLANE
SLOT = 6 * FIELD
PAD = 8 + 4 * PLANE
SHARP = stiffening * math.log2(math.e)
U_SCALE = fine_dt * relax_rate * 0.5
P_SCALE = U_SCALE * fine_dt * coupling * 0.5
GAIN = fine_dt * pressure_gain * relax_rate * 0.5 * P_SCALE / U_SCALE
MOVED = (0, 1, 2, 3, 5)


def lanes():
    return lax.broadcasted_iota(jnp.int32, (8, 128), 1)


def exchange_bits(v):
    lane = lanes()
    for b in range(2):
        high = ((lane >> (3 + b)) & 1) == 1
        step = 8 << b
        new = list(v)
        for i in range(4):
            if not (i >> b) & 1:
                j = i | (1 << b)
                new[i] = jnp.where(high, pltpu.roll(v[j], step, 1), v[i])
                new[j] = jnp.where(high, v[j], pltpu.roll(v[i], 128 - step, 1))
        v = new
    return v


def pack_kernel(ta_ref, disp, pres, poro, lab, mask, out, flat, big, win, rev):
    ta = ta_ref[0]
    zero = jnp.zeros((16, 128), F32)
    for f in range(7):
        field = disp[f] if f < 3 else (pres, poro, lab, mask)[f - 3][...].astype(F32)
        for h in range(2):
            flat[(f * 2 + h) * 64 : (f * 2 + h + 1) * 64, :] = field[:, h * 128 : (h + 1) * 128]

    def rows(f, h, xf):
        for xi in range(4):
            at = (f * 2 + h) * 64 + (4 + xi if xf else 3 - xi) * 8
            yield flat[at : at + 8, :]

    for t in range(4):
        one, two = 2 * t, min(2 * t + 1, 6)
        big[t * 288 : t * 288 + 16, :] = zero
        big[t * 288 + 272 : t * 288 + 288, :] = zero
        for h in range(2):
            parts = [part for xf in range(2) for f in (one, two) for part in rows(f, h, xf)]
            at = t * 288 + 16 + h * 128
            big[at : at + 128, :] = jnp.concatenate(parts, axis=0).T
        win[t * 64 : t * 64 + 64, :] = big[pl.ds(pl.multiple_of(t * 288 + ta * 32, 32), 64), :]
        for i in range(64):
            rev[t * 64 + i : t * 64 + i + 1, :] = win[t * 64 + 63 - i : t * 64 + 64 - i, :]
        win[256 + t * 64 : 320 + t * 64, :] = pltpu.roll(win[t * 64 : t * 64 + 64, :], 32, 1)
        rev[256 + t * 64 : 320 + t * 64, :] = pltpu.roll(rev[t * 64 : t * 64 + 64, :], 96, 1)
    near = (lax.broadcasted_iota(jnp.int32, (REACH, 128), 1) & 32) == 0
    for g in range(4):
        for f in range(7):
            t, odd = f // 2, f % 2
            low = 256 * odd + t * 64 + 44 - 8 * g
            high = 256 * (1 - odd) + t * 64 + 20 + 8 * g
            both = jnp.where(near, rev[low : low + REACH, :], win[high : high + REACH, :])
            out[g * ROWS + f * REACH : g * ROWS + (f + 1) * REACH, :] = both
        out[g * ROWS + 126 : g * ROWS + 128, :] = jnp.zeros((2, 128), F32)


def fold_kernel(recv, own, down, up):
    half0 = lanes() < 64

    def group(r, carry):
        def at(i):
            return pl.ds(pl.multiple_of(i * ROWS + r * 8, 8), 8)

        v = exchange_bits([recv[at(gy), :] for gy in range(4)])
        for i in range(4):
            own[at(i), :] = v[i]
        for i in range(2):
            down[at(i), :] = v[i]
            up[at(i), :] = v[i]
        down[at(2), :] = jnp.where(half0, v[2], pltpu.roll(v[3], 64, 1))
        up[at(2), :] = jnp.where(half0, pltpu.roll(v[3], 64, 1), v[2])
        return carry

    lax.fori_loop(0, ROWS // 8, group, 0)


def main_kernel(pos_ref, stiff_tab, cond_tab, own, east, west, east2, west2, out, a_st, b_st, c_st, t0, t1, raw, co, turn):
    lane = lanes()
    row = lax.broadcasted_iota(jnp.int32, (8, 128), 0)
    half0 = lane < 64
    near_z = (lane & 32) == 0
    y = lane & 31
    has_n, has_s = y < 31, y > 0
    zero = jnp.zeros((8, 128), F32)

    def swap_x(v):
        return pltpu.roll(v, 64, 1)

    def swap_z(v):
        return jnp.where(near_z, pltpu.roll(v, 96, 1), pltpu.roll(v, 32, 1))

    def tile(start):
        return pl.ds(pl.multiple_of(start, 8), 8)

    def spread(r, carry):
        def get(ref, i):
            return ref[tile(i * ROWS + r * 8), :]

        def place(xi, v):
            raw[pl.ds(r * (8 * PLANE) + xi, 8, stride=PLANE), :] = v

        for i in range(4):
            place(i, get(own, i))
            place(4 + i, swap_x(jnp.where(half0, get(east, 3 - i), get(west, 3 - i))))
            place(8 + i, jnp.where(half0, get(west, i), get(east, i)))
        for i in range(2):
            place(14 + i, swap_x(jnp.where(half0, get(east2, 1 - i), get(west2, 1 - i))))
            place(16 + i, jnp.where(half0, get(west2, i), get(east2, i)))
        e, w = get(east2, 2), get(west2, 2)
        place(13, swap_x(jnp.where(half0, e, w)))
        place(12, jnp.where(half0, w, e))
        for i in range(6):
            place(18 + i, zero)
        return carry

    lax.fori_loop(0, ROWS // 8, spread, 0)

    x0, z0 = pos_ref[0], pos_ref[1]

    def coefficients(zi, carry):
        z = jnp.where(near_z, z0 + 3 - zi, z0 + 4 + zi)
        in_z = (z >= 0) & (z < 256)
        for b in range(3):
            xi = row + 8 * b
            x = jnp.where(half0, x0 + 3 - xi, x0 + 4 + xi)
            here = in_z & (x >= 0) & (x < 64)
            label = raw[tile((5 * REACH + zi) * PLANE + 8 * b), :]
            drain = raw[tile((6 * REACH + zi) * PLANE + 8 * b), :]
            stiff, cond = zero, zero
            for i in range(6):
                hit = label == float(i)
                stiff = jnp.where(hit, stiff_tab[i], stiff)
                cond = jnp.where(hit, cond_tab[i], cond)
            stiff = jnp.where(here, stiff, 0.0)
            fine_a = stiff * fine_dt
            coarse_a = stiff * (fine_dt * FINE)
            values = (
                fine_a,
                1.0 - 6.0 * fine_a,
                coarse_a,
                1.0 - 6.0 * coarse_a,
                jnp.where(here, 1.0 - drain, 0.0),
                jnp.where(here, cond, -1.0e30),
                jnp.where(here, 1.0, 0.0).astype(F32),
            )
            for i, value in enumerate(values):
                co[tile(i * FIELD + (zi + 1) * PLANE + 8 + 8 * b), :] = value
        return carry

    lax.fori_loop(0, REACH, coefficients, 0)

    sign_x = jnp.where(half0, -U_SCALE, U_SCALE).astype(F32)
    sign_z = jnp.where(near_z, -U_SCALE, U_SCALE).astype(F32)

    def where_of(slot, zi, b0=0):
        return pl.multiple_of(slot * SLOT + (zi + 1) * PLANE + 8 + 8 * b0, 8)

    def load(ref, at, f, off=0):
        return ref[pl.ds(at + (f * FIELD + off), 8), :]

    def coef(at, i, off):
        return co[pl.ds(at + (i * FIELD + off), 8), :]

    def put(ref, at, off, vals, k=None):
        for f in range(5):
            ref[pl.ds(at + (f * FIELD + off), 8), :] = vals[f]
        if k is not None:
            ref[pl.ds(at + (5 * FIELD + off), 8), :] = k

    def conduct(ca, off, psi):
        return jnp.exp2(coef(ca, 5, off) - psi)

    def begin(zi, carry):
        at, ca = where_of(0, zi), where_of(0, zi)
        for b in range(3):
            vals = [raw[tile((f * REACH + zi) * PLANE + 8 * b), :] for f in range(5)]
            vals[0] = vals[0] * sign_x
            vals[1] = vals[1] * U_SCALE
            vals[2] = vals[2] * sign_z
            vals[3] = vals[3] * P_SCALE
            vals[4] = (1.0 - vals[4]) * SHARP
            k = conduct(ca, 8 * b, vals[4])
            for ref in (a_st, t1):
                put(ref, at, 8 * b, vals, k)
        return carry

    lax.fori_loop(0, REACH, begin, 0)

    def prepare(ref, at):
        for d in range(2):
            for b in range(2):
                for i, f in enumerate(MOVED):
                    v = load(ref, at, f, d * PLANE + 8 * b)
                    to = ((d * 2 + b) * 5 + i) * 16
                    turn[to : to + 8, :] = jnp.where(has_n, pltpu.roll(v, 127, 1), 0.0)
                    turn[to + 8 : to + 16, :] = jnp.where(has_s, pltpu.roll(v, 1, 1), 0.0)

    def advance(ref, slot, radius, fine, emit):
        units = (radius + 5) // 2
        passes = jnp.where(radius > 12, 2, 1)

        def unit(at, ca, carry, more):
            carry = list(carry)
            for d in range(2):
                for b in range(2):
                    off = d * PLANE + 8 * b
                    mid = {f: load(ref, at, f, off) for f in MOVED}
                    e = {f: load(ref, at, f, off + 1) for f in MOVED}
                    w = {f: load(ref, at, f, off - 1) for f in MOVED}
                    i = {f: load(ref, at, f, off + PLANE) for f in MOVED}
                    o = {f: load(ref, at, f, off - PLANE) for f in (0, 1, 2, 3)}
                    n, s = {}, {}
                    for j, f in enumerate(MOVED):
                        to = ((d * 2 + b) * 5 + j) * 16
                        n[f] = turn[to : to + 8, :]
                        s[f] = turn[to + 8 : to + 16, :]
                    p, k = mid[3], mid[5]
                    face = (i[5] + k) * (i[3] - p)
                    flux = face - carry[b]
                    carry[b] = face
                    for side in (e, w, n, s):
                        flux = flux + (side[5] + k) * (side[3] - p)
                    dil = (e[0] - w[0]) + (n[1] - s[1]) + (i[2] - o[2])
                    m = coef(ca, 6, off)
                    grads = [e[3] - w[3], n[3] - s[3], i[3] - o[3]]
                    gain = GAIN
                    if not fine:
                        m = m * float(FINE)
                        grads[1] = grads[1] * float(FINE)
                        flux = flux * float(FINE)
                        gain = GAIN * FINE
                    grads[0] = grads[0] * m
                    grads[2] = grads[2] * m
                    a = coef(ca, 0 if fine else 2, off)
                    a6 = coef(ca, 1 if fine else 3, off)
                    new = []
                    for f in range(3):
                        around = (e[f] + w[f]) + (n[f] + s[f]) + (i[f] + o[f])
                        new.append(a * around + a6 * mid[f] - grads[f])
                    new.append(coef(ca, 4, off) * (p + (flux - gain * dil)))
                    psi = load(ref, at, 4, off)
                    new.append(psi * (1.0 - (dil if fine else dil * float(FINE))))
                    emit(at - slot * SLOT, ca, off, new)
            if more:
                prepare(ref, pl.multiple_of(at + 2 * PLANE, 8))
            return tuple(carry)

        start = where_of(slot, 0)

        def ghost_x(f, zi):
            row0 = start + (f * FIELD + zi * PLANE)
            v = ref[pl.ds(row0, 8, stride=PLANE), :]
            ref[pl.ds(row0 - 1, 8, stride=PLANE), :] = swap_x(-v if f == 0 else v)

        def ghost_z(f, b):
            v = load(ref, start, f, 8 * b)
            v = swap_z(-v if f == 2 else v)
            ref[pl.ds(start + (f * FIELD + 8 * b - PLANE), 8), :] = v
            return v

        @pl.when(radius > 12)
        def _():
            for f in MOVED:
                ghost_z(f, 2)
                ghost_x(f, 10)

        def one_pass(j, c):
            b0 = passes - 1 - j
            at, ca = where_of(slot, 0, b0), where_of(0, 0, b0)
            for f in MOVED:
                ghost_x(f, 0)
                ghost_x(f, 8)
            for f in (0, 1, 2):
                for b in range(2):
                    ghost_z(f, b)
            carry = []
            for b in range(2):
                ghost_z(3, b)
                ghost_z(5, b)
            prepare(ref, at)
            for b in range(2):
                k0, k1 = load(ref, at, 5, 8 * b - PLANE), load(ref, at, 5, 8 * b)
                p0, p1 = load(ref, at, 3, 8 * b - PLANE), load(ref, at, 3, 8 * b)
                carry.append((k0 + k1) * (p1 - p0))

            def step(u, carry):
                shift = u * (2 * PLANE)
                return unit(pl.multiple_of(at + shift, 8), pl.multiple_of(ca + shift, 8), carry, True)

            carry = lax.fori_loop(0, units - 1, step, tuple(carry))
            shift = (units - 1) * (2 * PLANE)
            unit(pl.multiple_of(at + shift, 8), pl.multiple_of(ca + shift, 8), carry, False)
            return c

        lax.fori_loop(0, passes, one_pass, 0)

    def slot_at(slot, at):
        return pl.multiple_of(slot * SLOT + at, 8)

    def plain(src, slot, radius, fine, *targets):
        def emit(at, ca, off, new):
            k = conduct(ca, off, new[4])
            for ref, to in targets:
                put(ref, slot_at(to, at), off, new, k)

        advance(src, slot, radius, fine, emit)

    def minus(src, slot, radius, sub, to):
        def emit(at, ca, off, new):
            old = slot_at(sub, at)
            put(c_st, slot_at(to, at), off, [new[f] - load(a_st, old, f, off) for f in range(5)])

        advance(src, slot, radius, True, emit)

    def plus(src, radius, cor, keep, *targets):
        def emit(at, ca, off, new):
            if keep is not None:
                put(a_st, slot_at(keep, at), off, new)
            if targets:
                old = slot_at(cor, at)
                vals = [new[f] + load(c_st, old, f, off) for f in range(5)]
                k = conduct(ca, off, vals[4])
                for ref, to in targets:
                    put(ref, slot_at(to, at), off, vals, k)

        advance(src, 0, radius, False, emit)

    def fine_all(source, base, start):
        def slab(j, carry):
            plain(source, base + j, start - j, True, (t0, 0))
            plain(t0, 0, start - 1 - j, True, (t1, 0))
            plain(t1, 0, start - 2 - j, True, (t0, 0))
            minus(t0, 0, start - 3 - j, j + 1, j)

            @pl.when(j == 0)
            def _():
                for zi in range(4):
                    put(b_st, where_of(0, zi), 0, [load(b_st, where_of(1, zi), f) for f in range(5)])

                def body(zi, carry):
                    at = where_of(0, zi)
                    for b in range(2):
                        off = 8 * b
                        vals = [load(a_st, slot_at(1, at), f, off) + load(c_st, at, f, off) for f in range(5)]
                        put(b_st, slot_at(1, at), off, vals, conduct(at, off, vals[4]))
                    return carry

                lax.fori_loop(0, start + 1, body, 0)

            return carry

        lax.fori_loop(0, 7, slab, 0)

    def restart():
        def step(i, carry):
            for j in range(9):
                at = i * 72 + 8 * j
                t1[tile(at), :] = b_st[tile(SLOT + at), :]
            return carry

        lax.fori_loop(0, SLOT // 72, step, 0)

    def chain0(i, carry):
        k = 2 * i
        plain(t1, 0, 13 - k, False, (t0, 0), (a_st, k + 1))
        plain(t0, 0, 12 - k, False, (t1, 0), (a_st, k + 2))
        return carry

    lax.fori_loop(0, 3, chain0, 0)
    plain(t1, 0, jnp.int32(4), False, (a_st, 7))
    fine_all(a_st, 0, 13)
    restart()

    def chain1(i, carry):
        k = 2 * i + 1
        plus(t1, 10 - k, k, k, (t0, 0), (b_st, k + 1))
        plus(t0, 9 - k, k + 1, k + 1, (t1, 0), (b_st, k + 2))
        return carry

    lax.fori_loop(0, 3, chain1, 0)
    plus(t1, jnp.int32(0), None, 7)
    fine_all(b_st, 1, 9)
    restart()

    def chain2(i, carry):
        k = 2 * i + 2
        plus(t1, 7 - k, k - 1, None, (t0, 0), (b_st, k))
        plus(t0, 6 - k, k, None, (t1, 0), (b_st, k + 1))
        return carry

    lax.fori_loop(0, 3, chain2, 0)

    unsign_x = jnp.where(half0, -1.0 / U_SCALE, 1.0 / U_SCALE).astype(F32)
    unsign_z = jnp.where(near_z, -1.0 / U_SCALE, 1.0 / U_SCALE).astype(F32)
    for f in range(5):
        for zi in range(4):
            v = []
            for xi in range(4):
                e = b_st[pl.ds(f * FIELD + (zi + 1) * PLANE + 8 + xi, 8, stride=SLOT), :]
                if f == 4:
                    e = 1.0 - e * (1.0 / SHARP)
                else:
                    e = e * (unsign_x, 1.0 / U_SCALE, unsign_z, 1.0 / P_SCALE)[f]
                v.append(e)
            v = exchange_bits(v)
            for gy in range(4):
                out[pl.ds(gy * 24 + f * 4 + zi, 8, stride=96), :] = v[gy]
    for i in range(32):
        out[i * 24 + 20 : i * 24 + 24, :] = jnp.zeros((4, 128), F32)


def unpack_kernel(recv, out, rows):
    near_z = (lanes() & 32) == 0
    for t in range(3):
        for zi in range(4):
            for g in range(4):
                one = recv[pl.ds(g * 192 + 2 * t * 4 + zi, 8, stride=24), :]
                two = recv[pl.ds(g * 192 + min(2 * t + 1, 4) * 4 + zi, 8, stride=24), :]
                low = jnp.where(near_z, one, pltpu.roll(two, 32, 1))
                high = jnp.where(near_z, pltpu.roll(one, 96, 1), two)
                rows[pl.ds(t * 256 + g * 64 + 3 - zi, 8, stride=8), :] = low
                rows[pl.ds(t * 256 + g * 64 + 4 + zi, 8, stride=8), :] = high
        for h in range(2):
            block = rows[t * 256 + h * 128 : t * 256 + (h + 1) * 128, :].T
            for i in range(1 if t == 2 else 2):
                for xf in range(2):
                    for xi in range(4):
                        at = ((2 * t + i) * 8 + (4 + xi if xf else 3 - xi)) * 8
                        source = xf * 64 + i * 32 + xi * 8
                        out[at : at + 8, h * 128 : (h + 1) * 128] = block[source : source + 8, :]


def vmem():
    return pl.BlockSpec(memory_space=pltpu.VMEM)


def smem():
    return pl.BlockSpec(memory_space=pltpu.SMEM)


def scratch(rows):
    return pltpu.VMEM((rows, 128), F32)


def shaped(rows, width=128):
    return jax.ShapeDtypeStruct((rows, width), F32)


def pack(ta, *fields):
    return pl.pallas_call(
        pack_kernel,
        out_shape=shaped(4 * ROWS),
        in_specs=[smem()] + [vmem()] * 5,
        out_specs=vmem(),
        scratch_shapes=[scratch(896), scratch(1152), scratch(512), scratch(512)],
        interpret=INTERPRET,
        name="pack",
    )(ta, *fields)


def fold(recv):
    return pl.pallas_call(
        fold_kernel,
        out_shape=(shaped(4 * ROWS), shaped(3 * ROWS), shaped(3 * ROWS)),
        in_specs=[vmem()],
        out_specs=(vmem(), vmem(), vmem()),
        interpret=INTERPRET,
        name="fold",
    )(recv)


def compute(pos, stiff_table, perm_table, *blocks):
    cond_table = jnp.log2(perm_table) + (math.log2(0.5 * fine_dt) + SHARP * (1.0 - porosity_ref))
    return pl.pallas_call(
        main_kernel,
        out_shape=shaped(32 * 24),
        in_specs=[smem(), smem(), smem()] + [vmem()] * 5,
        out_specs=vmem(),
        scratch_shapes=[
            scratch(8 * SLOT + PAD),
            scratch(8 * SLOT + PAD),
            scratch(7 * SLOT + PAD),
            scratch(SLOT + PAD),
            scratch(SLOT + PAD),
            scratch(ROWS * PLANE),
            scratch(7 * FIELD + PAD),
            scratch(320),
        ],
        compiler_params=pltpu.CompilerParams(vmem_limit_bytes=58 << 20),
        interpret=INTERPRET,
        name="parareal",
    )(pos, stiff_table, cond_table, *blocks)


def unpack(recv):
    return pl.pallas_call(
        unpack_kernel,
        out_shape=shaped(320, 256),
        in_specs=[vmem()],
        out_specs=vmem(),
        scratch_shapes=[scratch(768)],
        interpret=INTERPRET,
        name="unpack",
    )(recv)


def shards(displacement, pressure, porosity, labels, ventricle_mask, stiff_table, perm_table):
    ta, gx, gy = (lax.axis_index(name).astype(jnp.int32) for name in ("ta", "gx", "gy"))
    flat = lambda a: a.reshape(a.shape[:-3] + (64, 256))
    sent = pack(
        ta.reshape(1), flat(displacement), flat(pressure), flat(porosity), flat(labels), flat(ventricle_mask)
    )
    got = lax.all_to_all(sent.reshape(4, ROWS, 128), "gy", 0, 0, tiled=True)
    own, down, up = fold(got.reshape(4 * ROWS, 128))

    def from_side(value, by):
        pairs = [(i, i - by) for i in range(8) if 0 <= i - by < 8]
        return lax.ppermute(value, "gx", pairs)

    blocks = (own, from_side(own, 1), from_side(own, -1), from_side(down, 2), from_side(up, -2))
    ends = compute(jnp.stack([gx * 8, ta * 32 + gy * 8]), stiff_table, perm_table, *blocks)
    mine = lax.all_to_all(ends.reshape(32, 24, 128), ("ta", "gy"), 0, 0, tiled=True)
    return unpack(mine.reshape(32 * 24, 128)).reshape(1, 5, 8, 8, 256)


def solution(mesh):
    placed = (
        P(None, "gx", "gy", None),
        P("gx", "gy", None),
        P("gx", "gy", None),
        P("gx", "gy", None),
        P("gx", "gy", None),
        P(),
        P(),
    )
    return jax.shard_map(
        shards,
        mesh=mesh,
        in_specs=placed,
        out_specs=P("ta", None, "gx", "gy", None),
        check_vma=False,
    )
```

time: 794 us -> 140 us (0.18); the launches traced: 781 us -> 140 us
  starting transfers between devices: 400 us -> 20.2 us
  waiting for transfers between devices: 354 us -> 14.6 us
  Pallas kernels: 0 us -> 78.4 us
  blocking collectives: 0 us -> 24.2 us
  other arithmetic: 22.9 us -> 1.14 us
    ppermute x137 -> x4, starting transfers between devices: 400 us -> 16.8 us  [from_side(): return lax.ppermute(value, 'gx', pairs)]
    ppermute x137 -> x4, waiting for transfers between devices: 354 us -> 8.63 us  [from_side(): return lax.ppermute(value, 'gx', pairs)]
    pallas_call x0 -> x4, Pallas kernels: none -> 78.4 us  [the longest x1 69.3 us: compute(): pl.pallas_call(main_kernel, out_shape=shaped(32 * 24), in_specs=[smem(),...]
    all_to_all x0 -> x1, blocking collectives: none -> 24.2 us  [shards(): lax.all_to_all(ends.reshape(32, 24, 128), ('ta', 'gy'), 0, 0, tiled=True)]
  transfers between devices with their start and end apart: 137 -> 5, of which waited for: 77 -> 3; matrix products, arithmetic and copies ran while one was open for 0% -> 1% of each run, Pallas kernels for 0% -> 0%
where the time goes in v2:
time: 140 us
  Pallas kernels  78.4 us (56%)
  blocking collectives  24.2 us (17%)
  starting transfers between devices  20.2 us (14%)
  waiting for transfers between devices  14.6 us (10%)
  local copies, waits for them, and re-layouts  1.41 us (1%)
    pallas_call x1, Pallas kernels, compute(): pl.pallas_call(main_kernel, out_shape=shaped(32 * 24), in_specs=[smem(),...  69.3 us
    all_to_all x1, blocking collectives, shards(): lax.all_to_all(ends.reshape(32, 24, 128), ('ta', 'gy'), 0, 0, tiled=True)  24.2 us
    ppermute x4, starting transfers between devices, from_side(): return lax.ppermute(value, 'gx', pairs)  16.8 us
    ppermute x4, waiting for transfers between devices, from_side(): return lax.ppermute(value, 'gx', pairs)  8.63 us
    all_to_all x1, waiting for transfers between devices, shards(): got = lax.all_to_all(sent.reshape(4, ROWS, 128), 'gy', 0, 0, tiled=True)  5.96 us
    pallas_call x1, Pallas kernels, fold(): pl.pallas_call(fold_kernel, out_shape=(shaped(4 * ROWS), shaped(3 * ROWS)...  5.05 us
    all_to_all x1, starting transfers between devices, shards(): got = lax.all_to_all(sent.reshape(4, ROWS, 128), 'gy', 0, 0, tiled=True)  3.41 us
  transfers between devices with their start and end apart: 5, of which 3 were waited for; matrix products, arithmetic and copies ran while one was open for 1% of the time, Pallas kernels for 0%

profile of v2, /device:TPU:6, one launch (start us, length us, event | category | flops | bytes accessed | tf_op | source)
XLA Modules:
  0.0 140.0 jit_solution(5870952968244057853)
XLA Ops:
  0.0 2.0 %pack.1 = f32[512,128]{1,0:T(8,128)} custom-call(s32[1]{0:T(128)} %bitcast.2.ta_ref, f32[3,64,256]{2,1,0:T(8,128)} %bitcast.17, f32[64,256]{1,0:T(8,128)} %bitcast.18, f32[64,256]{1,0:T(8,128)} %bitcast.19, s32[64,256]{1,0:T(8,128)} %bitcast.20, s32[64,256]{1,0:T(8,128)} %bitcast.21), custom_call_target="tpu_custom_call" | custom-call | tf_op jit(solution)/shard_map/pack/pallas_call | solution.py:483
  2.0 3.4 %all-to-all-start = ((f32[4,128,128]{2,1,0:T(8,128)}), f32[4,128,128]{2,1,0:T(8,128)S(1)}, u32[]{:S(2)}, u32[]{:S(2)}) async-start(f32[4,128,128]{2,1,0:T(8,128)} %bitcast.16), calls=%async_computation | async-start | bytes 524288 | tf_op jit(solution)/shard_map/all_to_all | solution.py:546
  5.5 6.0 %all-to-all-done = f32[4,128,128]{2,1,0:T(8,128)S(1)} async-done(((f32[4,128,128]{2,1,0:T(8,128)}), f32[4,128,128]{2,1,0:T(8,128)S(1)}, u32[]{:S(2)}, u32[]{:S(2)}) %all-to-all-start) | async-done | bytes 262176 | tf_op jit(solution)/shard_map/all_to_all | solution.py:546
  11.4 0.0 copy-start
  11.4 0.7 copy-done
  12.1 5.0 %fold.1 = (f32[512,128]{1,0:T(8,128)}, f32[384,128]{1,0:T(8,128)}, f32[384,128]{1,0:T(8,128)}) custom-call(f32[512,128]{1,0:T(8,128)} %bitcast.15), custom_call_target="tpu_custom_call" | custom-call | tf_op jit(solution)/shard_map/fold/pallas_call | solution.py:495
  17.2 5.0 %collective-permute-start.1 = (f32[512,128]{1,0:T(8,128)}, f32[512,128]{1,0:T(8,128)S(1)}, u32[]{:S(2)}, u32[]{:S(2)}) collective-permute-start(f32[512,128]{1,0:T(8,128)} %get-tuple-element.8.own), channel_id=1, source_target_pairs={{0,32},{32,64},{64,96},{96,128},{128,160},{160,192},{192,224},{1,3... | collective-permute-start | bytes 786440 | tf_op jit(solution)/shard_map/ppermute | solution.py:551
  22.2 1.9 %collective-permute-start = (f32[512,128]{1,0:T(8,128)}, f32[512,128]{1,0:T(8,128)S(1)}, u32[]{:S(2)}, u32[]{:S(2)}) collective-permute-start(f32[512,128]{1,0:T(8,128)} %get-tuple-element.8.own), channel_id=1, source_target_pairs={{32,0},{64,32},{96,64},{128,96},{160,128},{192,160},{224,192},{33,... | collective-permute-start | bytes 786440 | tf_op jit(solution)/shard_map/ppermute | solution.py:551
  24.1 0.6 pad_add_fusion.pos_ref
  24.7 0.0 copy-start.5
  24.7 2.3 %collective-permute-start.2 = (f32[384,128]{1,0:T(8,128)}, f32[384,128]{1,0:T(8,128)S(1)}, u32[]{:S(2)}, u32[]{:S(2)}) collective-permute-start(f32[384,128]{1,0:T(8,128)} %get-tuple-element.9), channel_id=1, source_target_pairs={{64,0},{96,32},{128,64},{160,96},{192,128},{224,160},{65,1},{97,33... | collective-permute-start | bytes 589832 | tf_op jit(solution)/shard_map/ppermute | solution.py:551
  27.1 7.5 %collective-permute-start.3 = (f32[384,128]{1,0:T(8,128)}, f32[384,128]{1,0:T(8,128)S(1)}, u32[]{:S(2)}, u32[]{:S(2)}) collective-permute-start(f32[384,128]{1,0:T(8,128)} %get-tuple-element.10), channel_id=1, source_target_pairs={{0,64},{32,96},{64,128},{96,160},{128,192},{160,224},{1,65},{33,97... | collective-permute-start | bytes 589832 | tf_op jit(solution)/shard_map/ppermute | solution.py:551
  34.6 0.0 copy-done.5
  34.6 0.5 multiply_add_fusion.cond_tab
  35.2 3.5 %collective-permute-done.2.east2 = f32[384,128]{1,0:T(8,128)S(1)} collective-permute-done((f32[384,128]{1,0:T(8,128)}, f32[384,128]{1,0:T(8,128)S(1)}, u32[]{:S(2)}, u32[]{:S(2)}) %collective-permute-start.2) | collective-permute-done | bytes 196640 | tf_op jit(solution)/shard_map/ppermute | solution.py:551
  38.7 0.0 copy-start.3
  38.7 0.0 collective-permute-done.3.west2
  38.7 0.0 copy-start.4
  38.7 0.0 collective-permute-done.1.west
  38.7 0.0 copy-start.1
  38.7 5.1 %collective-permute-done.east = f32[512,128]{1,0:T(8,128)S(1)} collective-permute-done((f32[512,128]{1,0:T(8,128)}, f32[512,128]{1,0:T(8,128)S(1)}, u32[]{:S(2)}, u32[]{:S(2)}) %collective-permute-start) | collective-permute-done | bytes 262176 | tf_op jit(solution)/shard_map/ppermute | solution.py:551
  43.8 0.0 copy-done.3
  43.8 0.0 copy-done.4
  43.8 0.0 copy-done.1
  43.8 0.0 copy-start.2
  43.8 0.7 copy-done.2
  44.5 69.3 %parareal.1 = f32[768,128]{1,0:T(8,128)} custom-call(s32[2]{0:T(128)} %pad_add_fusion.pos_ref, f32[6]{0:T(128)} %stiff_tab.1, f32[6]{0:T(128)} %multiply_add_fusion.cond_tab, f32[512,128]{1,0:T(8,128)} %get-tuple-element.8.own, f32[512,128]{1,0:T(8,128)} %copy-done.2, f32[512,128]{1,0:T(8,128)} %copy-done.1, f32[384,128]{1,0:T(8,128)} %copy-done.3, ...), custom_call_target="tpu_custom_call" | custom-call | tf_op jit(solution)/shard_map/parareal/pallas_call | solution.py:507
  113.8 24.2 %all_to_all.10 = f32[32,24,128]{2,1,0:T(8,128)} all-to-all(f32[32,24,128]{2,1,0:T(8,128)} %bitcast.13), channel_id=1, replica_groups=mesh['gx'=8,'gy'=4,'ta'=8] {'ta','gy'}, dimensions={0} | all-to-all | bytes 786432 | tf_op jit(solution)/shard_map/all_to_all | solution.py:555
  138.0 2.0 %unpack.1 = f32[320,256]{1,0:T(8,128)} custom-call(f32[768,128]{1,0:T(8,128)} %bitcast.14), custom_call_target="tpu_custom_call" | custom-call | tf_op jit(solution)/shard_map/unpack/pallas_call | solution.py:529
Async XLA Ops:
  2.0 9.4 %all-to-all-start = ((f32[4,128,128]{2,1,0:T(8,128)}), f32[4,128,128]{2,1,0:T(8,128)S(1)}, u32[]{:S(2)}, u32[]{:S(2)}) async-start(f32[4,128,128]{2,1,0:T(8,128)} %bitcast.16), calls=%async_computation | async-start | bytes 524288 | tf_op jit(solution)/shard_map/all_to_all | solution.py:546
  11.4 0.7 copy-start
  17.2 21.5 %collective-permute-start.1 = (f32[512,128]{1,0:T(8,128)}, f32[512,128]{1,0:T(8,128)S(1)}, u32[]{:S(2)}, u32[]{:S(2)}) collective-permute-start(f32[512,128]{1,0:T(8,128)} %get-tuple-element.8.own), channel_id=1, source_target_pairs={{0,32},{32,64},{64,96},{96,128},{128,160},{160,192},{192,224},{1,3... | collective-permute-start | bytes 786440 | tf_op jit(solution)/shard_map/ppermute | solution.py:551
  22.2 21.6 %collective-permute-start = (f32[512,128]{1,0:T(8,128)}, f32[512,128]{1,0:T(8,128)S(1)}, u32[]{:S(2)}, u32[]{:S(2)}) collective-permute-start(f32[512,128]{1,0:T(8,128)} %get-tuple-element.8.own), channel_id=1, source_target_pairs={{32,0},{64,32},{96,64},{128,96},{160,128},{192,160},{224,192},{33,... | collective-permute-start | bytes 786440 | tf_op jit(solution)/shard_map/ppermute | solution.py:551
  24.7 9.9 %copy-start.5 = (f32[6]{0:T(128)S(1)}, f32[6]{0:T(128)}, u32[]{:S(2)}) copy-start(f32[6]{0:T(128)} %param.13) | copy-start | bytes 76
  24.7 14.0 %collective-permute-start.2 = (f32[384,128]{1,0:T(8,128)}, f32[384,128]{1,0:T(8,128)S(1)}, u32[]{:S(2)}, u32[]{:S(2)}) collective-permute-start(f32[384,128]{1,0:T(8,128)} %get-tuple-element.9), channel_id=1, source_target_pairs={{64,0},{96,32},{128,64},{160,96},{192,128},{224,160},{65,1},{97,33... | collective-permute-start | bytes 589832 | tf_op jit(solution)/shard_map/ppermute | solution.py:551
  27.1 11.6 %collective-permute-start.3 = (f32[384,128]{1,0:T(8,128)}, f32[384,128]{1,0:T(8,128)S(1)}, u32[]{:S(2)}, u32[]{:S(2)}) collective-permute-start(f32[384,128]{1,0:T(8,128)} %get-tuple-element.10), channel_id=1, source_target_pairs={{0,64},{32,96},{64,128},{96,160},{128,192},{160,224},{1,65},{33,97... | collective-permute-start | bytes 589832 | tf_op jit(solution)/shard_map/ppermute | solution.py:551
  38.7 5.1 %copy-start.3 = (f32[384,128]{1,0:T(8,128)}, f32[384,128]{1,0:T(8,128)S(1)}, u32[]{:S(2)}) copy-start(f32[384,128]{1,0:T(8,128)S(1)} %collective-permute-done.2.east2) | copy-start | bytes 589828
  38.7 5.1 %copy-start.4 = (f32[384,128]{1,0:T(8,128)}, f32[384,128]{1,0:T(8,128)S(1)}, u32[]{:S(2)}) copy-start(f32[384,128]{1,0:T(8,128)S(1)} %collective-permute-done.3.west2) | copy-start | bytes 589828
  38.7 5.1 %copy-start.1 = (f32[512,128]{1,0:T(8,128)}, f32[512,128]{1,0:T(8,128)S(1)}, u32[]{:S(2)}) copy-start(f32[512,128]{1,0:T(8,128)S(1)} %collective-permute-done.1.west) | copy-start | bytes 786436
  43.8 0.7 copy-start.2

commit v3 on v2

--- a/solution.py
+++ b/solution.py
@@ -90,7 +90,7 @@
 def fold_kernel(recv, own, down, up):
     half0 = lanes() < 64
 
-    def group(r, carry):
+    def one(r):
         def at(i):
             return pl.ds(pl.multiple_of(i * ROWS + r * 8, 8), 8)
 
@@ -102,12 +102,16 @@
             up[at(i), :] = v[i]
         down[at(2), :] = jnp.where(half0, v[2], pltpu.roll(v[3], 64, 1))
         up[at(2), :] = jnp.where(half0, pltpu.roll(v[3], 64, 1), v[2])
-        return carry
-
-    lax.fori_loop(0, ROWS // 8, group, 0)
-
-
-def main_kernel(pos_ref, stiff_tab, cond_tab, own, east, west, east2, west2, out, a_st, b_st, c_st, t0, t1, raw, co, turn):
+
+    def group(r, carry):
+        for i in range(4):
+            one(r * 4 + i)
+        return carry
+
+    lax.fori_loop(0, ROWS // 32, group, 0)
+
+
+def main_kernel(pos_ref, stiff_tab, cond_tab, own, east, west, east2, west2, out, a_st, b_st, c_st, t0, t1, raw, co):
     lane = lanes()
     row = lax.broadcasted_iota(jnp.int32, (8, 128), 0)
     half0 = lane < 64
@@ -219,20 +223,17 @@
 
     lax.fori_loop(0, REACH, begin, 0)
 
-    def prepare(ref, at):
-        for d in range(2):
-            for b in range(2):
-                for i, f in enumerate(MOVED):
-                    v = load(ref, at, f, d * PLANE + 8 * b)
-                    to = ((d * 2 + b) * 5 + i) * 16
-                    turn[to : to + 8, :] = jnp.where(has_n, pltpu.roll(v, 127, 1), 0.0)
-                    turn[to + 8 : to + 16, :] = jnp.where(has_s, pltpu.roll(v, 1, 1), 0.0)
+    def north(v):
+        return jnp.where(has_n, pltpu.roll(v, 127, 1), 0.0)
+
+    def south(v):
+        return jnp.where(has_s, pltpu.roll(v, 1, 1), 0.0)
 
     def advance(ref, slot, radius, fine, emit):
         units = (radius + 5) // 2
         passes = jnp.where(radius > 12, 2, 1)
 
-        def unit(at, ca, carry, more):
+        def unit(at, ca, carry):
             carry = list(carry)
             for d in range(2):
                 for b in range(2):
@@ -244,9 +245,8 @@
                     o = {f: load(ref, at, f, off - PLANE) for f in (0, 1, 2, 3)}
                     n, s = {}, {}
                     for j, f in enumerate(MOVED):
-                        to = ((d * 2 + b) * 5 + j) * 16
-                        n[f] = turn[to : to + 8, :]
-                        s[f] = turn[to + 8 : to + 16, :]
+                        n[f] = north(mid[f])
+                        s[f] = south(mid[f])
                     p, k = mid[3], mid[5]
                     face = (i[5] + k) * (i[3] - p)
                     flux = face - carry[b]
@@ -274,8 +274,6 @@
                     psi = load(ref, at, 4, off)
                     new.append(psi * (1.0 - (dil if fine else dil * float(FINE))))
                     emit(at - slot * SLOT, ca, off, new)
-            if more:
-                prepare(ref, pl.multiple_of(at + 2 * PLANE, 8))
             return tuple(carry)
 
         start = where_of(slot, 0)
@@ -310,7 +308,6 @@
             for b in range(2):
                 ghost_z(3, b)
                 ghost_z(5, b)
-            prepare(ref, at)
             for b in range(2):
                 k0, k1 = load(ref, at, 5, 8 * b - PLANE), load(ref, at, 5, 8 * b)
                 p0, p1 = load(ref, at, 3, 8 * b - PLANE), load(ref, at, 3, 8 * b)
@@ -318,11 +315,9 @@
 
             def step(u, carry):
                 shift = u * (2 * PLANE)
-                return unit(pl.multiple_of(at + shift, 8), pl.multiple_of(ca + shift, 8), carry, True)
-
-            carry = lax.fori_loop(0, units - 1, step, tuple(carry))
-            shift = (units - 1) * (2 * PLANE)
-            unit(pl.multiple_of(at + shift, 8), pl.multiple_of(ca + shift, 8), carry, False)
+                return unit(pl.multiple_of(at + shift, 8), pl.multiple_of(ca + shift, 8), carry)
+
+            lax.fori_loop(0, units, step, tuple(carry))
             return c
 
         lax.fori_loop(0, passes, one_pass, 0)
@@ -486,6 +481,7 @@
         in_specs=[smem()] + [vmem()] * 5,
         out_specs=vmem(),
         scratch_shapes=[scratch(896), scratch(1152), scratch(512), scratch(512)],
+        compiler_params=pltpu.CompilerParams(vmem_limit_bytes=8 << 20),
         interpret=INTERPRET,
         name="pack",
     )(ta, *fields)
@@ -497,6 +493,7 @@
         out_shape=(shaped(4 * ROWS), shaped(3 * ROWS), shaped(3 * ROWS)),
         in_specs=[vmem()],
         out_specs=(vmem(), vmem(), vmem()),
+        compiler_params=pltpu.CompilerParams(vmem_limit_bytes=8 << 20),
         interpret=INTERPRET,
         name="fold",
     )(recv)
@@ -517,9 +514,8 @@
             scratch(SLOT + PAD),
             scratch(ROWS * PLANE),
             scratch(7 * FIELD + PAD),
-            scratch(320),
         ],
-        compiler_params=pltpu.CompilerParams(vmem_limit_bytes=58 << 20),
+        compiler_params=pltpu.CompilerParams(vmem_limit_bytes=42 << 20),
         interpret=INTERPRET,
         name="parareal",
     )(pos, stiff_table, cond_table, *blocks)
@@ -532,6 +528,7 @@
         in_specs=[vmem()],
         out_specs=vmem(),
         scratch_shapes=[scratch(768)],
+        compiler_params=pltpu.CompilerParams(vmem_limit_bytes=8 << 20),
         interpret=INTERPRET,
         name="unpack",
     )(recv)

time: 140 us -> 132 us (0.943)
  Pallas kernels: 78.4 us -> 67.3 us
  local copies, waits for them, and re-layouts: 1.41 us -> 4.29 us
    pallas_call x1, Pallas kernels: 69.3 us -> 64.5 us  [compute(): pl.pallas_call(main_kernel, out_shape=shaped(32 * 24), in_specs=[smem(),...]
    pallas_call x1, Pallas kernels: 5.05 us -> 0.85 us  [fold(): pl.pallas_call(fold_kernel, out_shape=(shaped(4 * ROWS), shaped(3 * ROWS)...]
    unnamed x12 -> x14, local copies, waits for them, and re-layouts: 1.41 us -> 4.29 us
  transfers between devices with their start and end apart: 5 -> 5, of which waited for: 3 -> 3; matrix products, arithmetic and copies ran while one was open for 1% -> 0% of each run, Pallas kernels for 0% -> 0%
where the time goes in v3:
time: 132 us; the launch traced here: 131 us
  Pallas kernels  67.3 us (51%)
  blocking collectives  23.9 us (18%)
  starting transfers between devices  20.2 us (15%)
  waiting for transfers between devices  15.4 us (12%)
  local copies, waits for them, and re-layouts  4.29 us (3%)
    pallas_call x1, Pallas kernels, compute(): pl.pallas_call(main_kernel, out_shape=shaped(32 * 24), in_specs=[smem(),...  64.5 us
    all_to_all x1, blocking collectives, shards(): lax.all_to_all(ends.reshape(32, 24, 128), ('ta', 'gy'), 0, 0, tiled=True)  23.9 us
    ppermute x4, starting transfers between devices, from_side(): return lax.ppermute(value, 'gx', pairs)  16.8 us
    ppermute x4, waiting for transfers between devices, from_side(): return lax.ppermute(value, 'gx', pairs)  9.47 us
    all_to_all x1, waiting for transfers between devices, shards(): got = lax.all_to_all(sent.reshape(4, ROWS, 128), 'gy', 0, 0, tiled=True)  5.96 us
    unnamed x14, local copies, waits for them, and re-layouts  4.29 us
    all_to_all x1, starting transfers between devices, shards(): got = lax.all_to_all(sent.reshape(4, ROWS, 128), 'gy', 0, 0, tiled=True)  3.41 us
  transfers between devices with their start and end apart: 5, of which 3 were waited for; matrix products, arithmetic and copies ran while one was open for 0% of the time, Pallas kernels for 0%

profile of v3, /device:TPU:6, one launch (start us, length us, event | category | flops | bytes accessed | tf_op | source)
XLA Modules:
  0.0 131.3 jit_solution(3685725801073287610)
XLA Ops:
  0.0 0.0 copy-start
  0.0 0.9 copy-done
  0.9 0.0 copy-start.1
  0.9 0.8 copy-done.1
  1.8 0.0 copy-start.2
  1.8 0.8 copy-done.2
  2.6 0.0 copy-start.3
  2.6 0.8 copy-done.3
  3.4 0.0 copy-start.4
  3.5 0.8 copy-done.4
  4.3 1.0 pack.1
  5.3 3.4 %all-to-all-start = ((f32[4,128,128]{2,1,0:T(8,128)}), f32[4,128,128]{2,1,0:T(8,128)S(1)}, u32[]{:S(2)}, u32[]{:S(2)}) async-start(f32[4,128,128]{2,1,0:T(8,128)} %bitcast.8), calls=%async_computation | async-start | bytes 524288 | tf_op jit(solution)/shard_map/all_to_all | solution.py:543
  8.7 6.0 %all-to-all-done = f32[4,128,128]{2,1,0:T(8,128)S(1)} async-done(((f32[4,128,128]{2,1,0:T(8,128)}), f32[4,128,128]{2,1,0:T(8,128)S(1)}, u32[]{:S(2)}, u32[]{:S(2)}) %all-to-all-start) | async-done | bytes 262176 | tf_op jit(solution)/shard_map/all_to_all | solution.py:543
  14.7 0.9 fold.1
  15.5 5.0 %collective-permute-start.1 = (f32[512,128]{1,0:T(8,128)S(1)}, f32[512,128]{1,0:T(8,128)S(1)}, u32[]{:S(2)}, u32[]{:S(2)}) collective-permute-start(f32[512,128]{1,0:T(8,128)S(1)} %get-tuple-element.8.own), channel_id=1, source_target_pairs={{0,32},{32,64},{64,96},{96,128},{128,160},{160,192},{192,224},{1,3... | collective-permute-start | bytes 786440 | tf_op jit(solution)/shard_map/ppermute | solution.py:548
  20.6 1.9 %collective-permute-start = (f32[512,128]{1,0:T(8,128)S(1)}, f32[512,128]{1,0:T(8,128)S(1)}, u32[]{:S(2)}, u32[]{:S(2)}) collective-permute-start(f32[512,128]{1,0:T(8,128)S(1)} %get-tuple-element.8.own), channel_id=1, source_target_pairs={{32,0},{64,32},{96,64},{128,96},{160,128},{192,160},{224,192},{33,... | collective-permute-start | bytes 786440 | tf_op jit(solution)/shard_map/ppermute | solution.py:548
  22.5 0.1 pad_add_fusion.pos_ref
  22.6 0.0 copy-start.6
  22.6 2.4 %collective-permute-start.2 = (f32[384,128]{1,0:T(8,128)S(1)}, f32[384,128]{1,0:T(8,128)S(1)}, u32[]{:S(2)}, u32[]{:S(2)}) collective-permute-start(f32[384,128]{1,0:T(8,128)S(1)} %get-tuple-element.9), channel_id=1, source_target_pairs={{64,0},{96,32},{128,64},{160,96},{192,128},{224,160},{65,1},{97,33... | collective-permute-start | bytes 589832 | tf_op jit(solution)/shard_map/ppermute | solution.py:548
  24.9 0.0 copy-start.5
  24.9 7.5 %collective-permute-start.3 = (f32[384,128]{1,0:T(8,128)S(1)}, f32[384,128]{1,0:T(8,128)S(1)}, u32[]{:S(2)}, u32[]{:S(2)}) collective-permute-start(f32[384,128]{1,0:T(8,128)S(1)} %get-tuple-element.10), channel_id=1, source_target_pairs={{0,64},{32,96},{64,128},{96,160},{128,192},{160,224},{1,65},{33,97... | collective-permute-start | bytes 589832 | tf_op jit(solution)/shard_map/ppermute | solution.py:548
  32.5 0.0 copy-done.6
  32.5 3.9 %collective-permute-done.2.east2 = f32[384,128]{1,0:T(8,128)S(1)} collective-permute-done((f32[384,128]{1,0:T(8,128)S(1)}, f32[384,128]{1,0:T(8,128)S(1)}, u32[]{:S(2)}, u32[]{:S(2)}) %collective-permute-start.2) | collective-permute-done | bytes 196640 | tf_op jit(solution)/shard_map/ppermute | solution.py:548
  36.4 0.0 collective-permute-done.3.west2
  36.4 0.0 collective-permute-done.1.west
  36.4 5.6 %collective-permute-done.east = f32[512,128]{1,0:T(8,128)S(1)} collective-permute-done((f32[512,128]{1,0:T(8,128)S(1)}, f32[512,128]{1,0:T(8,128)S(1)}, u32[]{:S(2)}, u32[]{:S(2)}) %collective-permute-start) | collective-permute-done | bytes 262176 | tf_op jit(solution)/shard_map/ppermute | solution.py:548
  42.0 0.0 copy-done.5
  42.0 64.5 %parareal.1 = f32[768,128]{1,0:T(8,128)S(1)} custom-call(s32[2]{0:T(128)S(1)} %pad_add_fusion.pos_ref, f32[6]{0:T(128)S(1)} %copy-done.5, f32[6]{0:T(128)S(1)} %multiply_add_fusion.cond_tab, f32[512,128]{1,0:T(8,128)S(1)} %get-tuple-element.8.own, f32[512,128]{1,0:T(8,128)S(1)} %collective-permute-done.east, f32[512,128]{1,0:T(8,128)S(1)} %collective-permute-done.1.west, ...), custom_call_target="tpu_custom_call" | custom-call | tf_op jit(solution)/shard_map/parareal/pallas_call | solution.py:504
  106.4 23.9 %all_to_all.10 = f32[32,24,128]{2,1,0:T(8,128)S(1)} all-to-all(f32[32,24,128]{2,1,0:T(8,128)S(1)} %bitcast.13), channel_id=1, replica_groups=mesh['gx'=8,'gy'=4,'ta'=8] {'ta','gy'}, dimensions={0} | all-to-all | bytes 786432 | tf_op jit(solution)/shard_map/all_to_all | solution.py:552
  130.3 1.0 unpack.1
  (1 shorter events, 0.0 us)
Async XLA Ops:
  0.0 0.9 copy-start
  0.9 0.8 copy-start.1
  1.8 0.8 copy-start.2
  2.6 0.8 copy-start.3
  3.4 0.8 copy-start.4
  5.3 9.4 %all-to-all-start = ((f32[4,128,128]{2,1,0:T(8,128)}), f32[4,128,128]{2,1,0:T(8,128)S(1)}, u32[]{:S(2)}, u32[]{:S(2)}) async-start(f32[4,128,128]{2,1,0:T(8,128)} %bitcast.8), calls=%async_computation | async-start | bytes 524288 | tf_op jit(solution)/shard_map/all_to_all | solution.py:543
  15.5 20.8 %collective-permute-start.1 = (f32[512,128]{1,0:T(8,128)S(1)}, f32[512,128]{1,0:T(8,128)S(1)}, u32[]{:S(2)}, u32[]{:S(2)}) collective-permute-start(f32[512,128]{1,0:T(8,128)S(1)} %get-tuple-element.8.own), channel_id=1, source_target_pairs={{0,32},{32,64},{64,96},{96,128},{128,160},{160,192},{192,224},{1,3... | collective-permute-start | bytes 786440 | tf_op jit(solution)/shard_map/ppermute | solution.py:548
  20.6 21.4 %collective-permute-start = (f32[512,128]{1,0:T(8,128)S(1)}, f32[512,128]{1,0:T(8,128)S(1)}, u32[]{:S(2)}, u32[]{:S(2)}) collective-permute-start(f32[512,128]{1,0:T(8,128)S(1)} %get-tuple-element.8.own), channel_id=1, source_target_pairs={{32,0},{64,32},{96,64},{128,96},{160,128},{192,160},{224,192},{33,... | collective-permute-start | bytes 786440 | tf_op jit(solution)/shard_map/ppermute | solution.py:548
  22.6 9.9 %copy-start.6 = (f32[6]{0:T(128)S(1)}, f32[6]{0:T(128)}, u32[]{:S(2)}) copy-start(f32[6]{0:T(128)} %param.13) | copy-start | bytes 76
  22.6 13.8 %collective-permute-start.2 = (f32[384,128]{1,0:T(8,128)S(1)}, f32[384,128]{1,0:T(8,128)S(1)}, u32[]{:S(2)}, u32[]{:S(2)}) collective-permute-start(f32[384,128]{1,0:T(8,128)S(1)} %get-tuple-element.9), channel_id=1, source_target_pairs={{64,0},{96,32},{128,64},{160,96},{192,128},{224,160},{65,1},{97,33... | collective-permute-start | bytes 589832 | tf_op jit(solution)/shard_map/ppermute | solution.py:548
  24.9 17.0 %copy-start.5 = (f32[6]{0:T(128)S(1)}, f32[6]{0:T(128)}, u32[]{:S(2)}) copy-start(f32[6]{0:T(128)} %stiff_tab.1) | copy-start | bytes 76
  24.9 11.4 %collective-permute-start.3 = (f32[384,128]{1,0:T(8,128)S(1)}, f32[384,128]{1,0:T(8,128)S(1)}, u32[]{:S(2)}, u32[]{:S(2)}) collective-permute-start(f32[384,128]{1,0:T(8,128)S(1)} %get-tuple-element.10), channel_id=1, source_target_pairs={{0,64},{32,96},{64,128},{96,160},{128,192},{160,224},{1,65},{33,97... | collective-permute-start | bytes 589832 | tf_op jit(solution)/shard_map/ppermute | solution.py:548

commit v4 on v3

--- a/solution.py
+++ b/solution.py
@@ -313,11 +313,19 @@
                 p0, p1 = load(ref, at, 3, 8 * b - PLANE), load(ref, at, 3, 8 * b)
                 carry.append((k0 + k1) * (p1 - p0))
 
-            def step(u, carry):
+            def moved(u, carry):
                 shift = u * (2 * PLANE)
                 return unit(pl.multiple_of(at + shift, 8), pl.multiple_of(ca + shift, 8), carry)
 
-            lax.fori_loop(0, units, step, tuple(carry))
+            def two(u, carry):
+                return moved(2 * u + 1, moved(2 * u, carry))
+
+            carry = lax.fori_loop(0, units // 2, two, tuple(carry))
+
+            @pl.when(units % 2 == 1)
+            def _():
+                moved(units - 1, carry)
+
             return c
 
         lax.fori_loop(0, passes, one_pass, 0)
@@ -432,9 +440,7 @@
                 v.append(e)
             v = exchange_bits(v)
             for gy in range(4):
-                out[pl.ds(gy * 24 + f * 4 + zi, 8, stride=96), :] = v[gy]
-    for i in range(32):
-        out[i * 24 + 20 : i * 24 + 24, :] = jnp.zeros((4, 128), F32)
+                out[pl.ds(gy * 20 + f * 4 + zi, 8, stride=80), :] = v[gy]
 
 
 def unpack_kernel(recv, out, rows):
@@ -442,8 +448,8 @@
     for t in range(3):
         for zi in range(4):
             for g in range(4):
-                one = recv[pl.ds(g * 192 + 2 * t * 4 + zi, 8, stride=24), :]
-                two = recv[pl.ds(g * 192 + min(2 * t + 1, 4) * 4 + zi, 8, stride=24), :]
+                one = recv[pl.ds(g * 160 + 2 * t * 4 + zi, 8, stride=20), :]
+                two = recv[pl.ds(g * 160 + min(2 * t + 1, 4) * 4 + zi, 8, stride=20), :]
                 low = jnp.where(near_z, one, pltpu.roll(two, 32, 1))
                 high = jnp.where(near_z, pltpu.roll(one, 96, 1), two)
                 rows[pl.ds(t * 256 + g * 64 + 3 - zi, 8, stride=8), :] = low
@@ -481,7 +487,6 @@
         in_specs=[smem()] + [vmem()] * 5,
         out_specs=vmem(),
         scratch_shapes=[scratch(896), scratch(1152), scratch(512), scratch(512)],
-        compiler_params=pltpu.CompilerParams(vmem_limit_bytes=8 << 20),
         interpret=INTERPRET,
         name="pack",
     )(ta, *fields)
@@ -503,7 +508,7 @@
     cond_table = jnp.log2(perm_table) + (math.log2(0.5 * fine_dt) + SHARP * (1.0 - porosity_ref))
     return pl.pallas_call(
         main_kernel,
-        out_shape=shaped(32 * 24),
+        out_shape=shaped(32 * 20),
         in_specs=[smem(), smem(), smem()] + [vmem()] * 5,
         out_specs=vmem(),
         scratch_shapes=[
@@ -549,8 +554,8 @@
 
     blocks = (own, from_side(own, 1), from_side(own, -1), from_side(down, 2), from_side(up, -2))
     ends = compute(jnp.stack([gx * 8, ta * 32 + gy * 8]), stiff_table, perm_table, *blocks)
-    mine = lax.all_to_all(ends.reshape(32, 24, 128), ("ta", "gy"), 0, 0, tiled=True)
-    return unpack(mine.reshape(32 * 24, 128)).reshape(1, 5, 8, 8, 256)
+    mine = lax.all_to_all(ends.reshape(32, 5, 4, 128), ("ta", "gy"), 0, 0, tiled=True)
+    return unpack(mine.reshape(32 * 20, 128)).reshape(1, 5, 8, 8, 256)
 
 
 def solution(mesh):

time: 132 us -> 113 us (0.86)
  Pallas kernels: 67.3 us -> 54.7 us
  local copies, waits for them, and re-layouts: 4.29 us -> 0.01 us
  blocking collectives: 23.9 us -> 22.4 us
    pallas_call x1, Pallas kernels: 64.5 us -> 50.8 us  [compute(): pl.pallas_call(main_kernel, out_shape=shaped(32 * 20), in_specs=[smem(),...]
    unnamed x14 -> x4, local copies, waits for them, and re-layouts: 4.29 us -> 0.01 us
    all_to_all x1, blocking collectives: 23.9 us -> 22.4 us  [shards(): lax.all_to_all(ends.reshape(32, 5, 4, 128), ('ta', 'gy'), 0, 0, tiled=True)]
where the time goes in v4:
time: 113 us
  Pallas kernels  54.7 us (48%)
  blocking collectives  22.4 us (20%)
  starting transfers between devices  20.2 us (18%)
  waiting for transfers between devices  15.4 us (14%)
    pallas_call x1, Pallas kernels, compute(): pl.pallas_call(main_kernel, out_shape=shaped(32 * 20), in_specs=[smem(),...  50.8 us
    all_to_all x1, blocking collectives, shards(): lax.all_to_all(ends.reshape(32, 5, 4, 128), ('ta', 'gy'), 0, 0, tiled=True)  22.4 us
    ppermute x4, starting transfers between devices, from_side(): return lax.ppermute(value, 'gx', pairs)  16.8 us
    ppermute x4, waiting for transfers between devices, from_side(): return lax.ppermute(value, 'gx', pairs)  9.47 us
    all_to_all x1, waiting for transfers between devices, shards(): got = lax.all_to_all(sent.reshape(4, ROWS, 128), 'gy', 0, 0, tiled=True)  5.96 us
    all_to_all x1, starting transfers between devices, shards(): got = lax.all_to_all(sent.reshape(4, ROWS, 128), 'gy', 0, 0, tiled=True)  3.41 us
  transfers between devices with their start and end apart: 5, of which 3 were waited for; matrix products, arithmetic and copies ran while one was open for 0% of the time, Pallas kernels for 0%

profile of v4, /device:TPU:6, one launch (start us, length us, event | category | flops | bytes accessed | tf_op | source)
XLA Modules:
  0.0 113.0 jit_solution(16629597749094330021)
XLA Ops:
  0.0 2.0 %pack.1 = f32[512,128]{1,0:T(8,128)} custom-call(s32[1]{0:T(128)} %bitcast.2.ta_ref, f32[3,64,256]{2,1,0:T(8,128)} %bitcast.17, f32[64,256]{1,0:T(8,128)} %bitcast.18, f32[64,256]{1,0:T(8,128)} %bitcast.19, s32[64,256]{1,0:T(8,128)} %bitcast.20, s32[64,256]{1,0:T(8,128)} %bitcast.21), custom_call_target="tpu_custom_call" | custom-call | tf_op jit(solution)/shard_map/pack/pallas_call | solution.py:484
  2.0 3.4 %all-to-all-start = ((f32[4,128,128]{2,1,0:T(8,128)}), f32[4,128,128]{2,1,0:T(8,128)S(1)}, u32[]{:S(2)}, u32[]{:S(2)}) async-start(f32[4,128,128]{2,1,0:T(8,128)} %bitcast.16), calls=%async_computation | async-start | bytes 524288 | tf_op jit(solution)/shard_map/all_to_all | solution.py:548
  5.5 6.0 %all-to-all-done = f32[4,128,128]{2,1,0:T(8,128)S(1)} async-done(((f32[4,128,128]{2,1,0:T(8,128)}), f32[4,128,128]{2,1,0:T(8,128)S(1)}, u32[]{:S(2)}, u32[]{:S(2)}) %all-to-all-start) | async-done | bytes 262176 | tf_op jit(solution)/shard_map/all_to_all | solution.py:548
  11.4 0.9 fold.1
  12.3 5.0 %collective-permute-start.1 = (f32[512,128]{1,0:T(8,128)S(1)}, f32[512,128]{1,0:T(8,128)S(1)}, u32[]{:S(2)}, u32[]{:S(2)}) collective-permute-start(f32[512,128]{1,0:T(8,128)S(1)} %get-tuple-element.8.own), channel_id=1, source_target_pairs={{0,32},{32,64},{64,96},{96,128},{128,160},{160,192},{192,224},{1,3... | collective-permute-start | bytes 786440 | tf_op jit(solution)/shard_map/ppermute | solution.py:553
  17.3 1.9 %collective-permute-start = (f32[512,128]{1,0:T(8,128)S(1)}, f32[512,128]{1,0:T(8,128)S(1)}, u32[]{:S(2)}, u32[]{:S(2)}) collective-permute-start(f32[512,128]{1,0:T(8,128)S(1)} %get-tuple-element.8.own), channel_id=1, source_target_pairs={{32,0},{64,32},{96,64},{128,96},{160,128},{192,160},{224,192},{33,... | collective-permute-start | bytes 786440 | tf_op jit(solution)/shard_map/ppermute | solution.py:553
  19.2 0.1 pad_add_fusion.pos_ref
  19.3 0.0 copy-start.1
  19.3 2.4 %collective-permute-start.2 = (f32[384,128]{1,0:T(8,128)S(1)}, f32[384,128]{1,0:T(8,128)S(1)}, u32[]{:S(2)}, u32[]{:S(2)}) collective-permute-start(f32[384,128]{1,0:T(8,128)S(1)} %get-tuple-element.9), channel_id=1, source_target_pairs={{64,0},{96,32},{128,64},{160,96},{192,128},{224,160},{65,1},{97,33... | collective-permute-start | bytes 589832 | tf_op jit(solution)/shard_map/ppermute | solution.py:553
  21.7 0.0 copy-start
  21.7 7.5 %collective-permute-start.3 = (f32[384,128]{1,0:T(8,128)S(1)}, f32[384,128]{1,0:T(8,128)S(1)}, u32[]{:S(2)}, u32[]{:S(2)}) collective-permute-start(f32[384,128]{1,0:T(8,128)S(1)} %get-tuple-element.10), channel_id=1, source_target_pairs={{0,64},{32,96},{64,128},{96,160},{128,192},{160,224},{1,65},{33,97... | collective-permute-start | bytes 589832 | tf_op jit(solution)/shard_map/ppermute | solution.py:553
  29.2 0.0 copy-done.1
  29.2 3.9 %collective-permute-done.2.east2 = f32[384,128]{1,0:T(8,128)S(1)} collective-permute-done((f32[384,128]{1,0:T(8,128)S(1)}, f32[384,128]{1,0:T(8,128)S(1)}, u32[]{:S(2)}, u32[]{:S(2)}) %collective-permute-start.2) | collective-permute-done | bytes 196640 | tf_op jit(solution)/shard_map/ppermute | solution.py:553
  33.1 0.0 collective-permute-done.3.west2
  33.1 0.0 collective-permute-done.1.west
  33.1 5.6 %collective-permute-done.east = f32[512,128]{1,0:T(8,128)S(1)} collective-permute-done((f32[512,128]{1,0:T(8,128)S(1)}, f32[512,128]{1,0:T(8,128)S(1)}, u32[]{:S(2)}, u32[]{:S(2)}) %collective-permute-start) | collective-permute-done | bytes 262176 | tf_op jit(solution)/shard_map/ppermute | solution.py:553
  38.7 0.0 copy-done
  38.7 50.8 %parareal.1 = f32[640,128]{1,0:T(8,128)S(1)} custom-call(s32[2]{0:T(128)S(1)} %pad_add_fusion.pos_ref, f32[6]{0:T(128)S(1)} %copy-done, f32[6]{0:T(128)S(1)} %multiply_add_fusion.cond_tab, f32[512,128]{1,0:T(8,128)S(1)} %get-tuple-element.8.own, f32[512,128]{1,0:T(8,128)S(1)} %collective-permute-done.east, f32[512,128]{1,0:T(8,128)S(1)} %collective-permute-done.1.west, ...), custom_call_target="tpu_custom_call" | custom-call | tf_op jit(solution)/shard_map/parareal/pallas_call | solution.py:509
  89.5 22.4 %all_to_all.10 = f32[32,5,4,128]{3,2,1,0:T(4,128)S(1)} all-to-all(f32[32,5,4,128]{3,2,1,0:T(4,128)S(1)} %bitcast.14), channel_id=1, replica_groups=mesh['gx'=8,'gy'=4,'ta'=8] {'ta','gy'}, dimensions={0} | all-to-all | bytes 655360 | tf_op jit(solution)/shard_map/all_to_all | solution.py:557
  112.0 1.0 unpack.1
  (1 shorter events, 0.0 us)
Async XLA Ops:
  2.0 9.4 %all-to-all-start = ((f32[4,128,128]{2,1,0:T(8,128)}), f32[4,128,128]{2,1,0:T(8,128)S(1)}, u32[]{:S(2)}, u32[]{:S(2)}) async-start(f32[4,128,128]{2,1,0:T(8,128)} %bitcast.16), calls=%async_computation | async-start | bytes 524288 | tf_op jit(solution)/shard_map/all_to_all | solution.py:548
  12.3 20.8 %collective-permute-start.1 = (f32[512,128]{1,0:T(8,128)S(1)}, f32[512,128]{1,0:T(8,128)S(1)}, u32[]{:S(2)}, u32[]{:S(2)}) collective-permute-start(f32[512,128]{1,0:T(8,128)S(1)} %get-tuple-element.8.own), channel_id=1, source_target_pairs={{0,32},{32,64},{64,96},{96,128},{128,160},{160,192},{192,224},{1,3... | collective-permute-start | bytes 786440 | tf_op jit(solution)/shard_map/ppermute | solution.py:553
  17.3 21.4 %collective-permute-start = (f32[512,128]{1,0:T(8,128)S(1)}, f32[512,128]{1,0:T(8,128)S(1)}, u32[]{:S(2)}, u32[]{:S(2)}) collective-permute-start(f32[512,128]{1,0:T(8,128)S(1)} %get-tuple-element.8.own), channel_id=1, source_target_pairs={{32,0},{64,32},{96,64},{128,96},{160,128},{192,160},{224,192},{33,... | collective-permute-start | bytes 786440 | tf_op jit(solution)/shard_map/ppermute | solution.py:553
  19.3 9.9 %copy-start.1 = (f32[6]{0:T(128)S(1)}, f32[6]{0:T(128)}, u32[]{:S(2)}) copy-start(f32[6]{0:T(128)} %param.13) | copy-start | bytes 76
  19.3 13.8 %collective-permute-start.2 = (f32[384,128]{1,0:T(8,128)S(1)}, f32[384,128]{1,0:T(8,128)S(1)}, u32[]{:S(2)}, u32[]{:S(2)}) collective-permute-start(f32[384,128]{1,0:T(8,128)S(1)} %get-tuple-element.9), channel_id=1, source_target_pairs={{64,0},{96,32},{128,64},{160,96},{192,128},{224,160},{65,1},{97,33... | collective-permute-start | bytes 589832 | tf_op jit(solution)/shard_map/ppermute | solution.py:553
  21.7 17.0 %copy-start = (f32[6]{0:T(128)S(1)}, f32[6]{0:T(128)}, u32[]{:S(2)}) copy-start(f32[6]{0:T(128)} %stiff_tab.1) | copy-start | bytes 76
  21.7 11.4 %collective-permute-start.3 = (f32[384,128]{1,0:T(8,128)S(1)}, f32[384,128]{1,0:T(8,128)S(1)}, u32[]{:S(2)}, u32[]{:S(2)}) collective-permute-start(f32[384,128]{1,0:T(8,128)S(1)} %get-tuple-element.10), channel_id=1, source_target_pairs={{0,64},{32,96},{64,128},{96,160},{128,192},{160,224},{1,65},{33,97... | collective-permute-start | bytes 589832 | tf_op jit(solution)/shard_map/ppermute | solution.py:553

commit v5 on v4

--- a/solution.py
+++ b/solution.py
@@ -20,6 +20,7 @@
 
 REACH = 18
 ROWS = 128
+FAR = 64
 PLANE = 24
 FIELD = 19 * PLANE
 SLOT = 6 * FIELD
@@ -87,7 +88,7 @@
         out[g * ROWS + 126 : g * ROWS + 128, :] = jnp.zeros((2, 128), F32)
 
 
-def fold_kernel(recv, own, down, up):
+def fold_kernel(recv, own, down, up, mix_d, mix_u):
     half0 = lanes() < 64
 
     def one(r):
@@ -97,11 +98,8 @@
         v = exchange_bits([recv[at(gy), :] for gy in range(4)])
         for i in range(4):
             own[at(i), :] = v[i]
-        for i in range(2):
-            down[at(i), :] = v[i]
-            up[at(i), :] = v[i]
-        down[at(2), :] = jnp.where(half0, v[2], pltpu.roll(v[3], 64, 1))
-        up[at(2), :] = jnp.where(half0, pltpu.roll(v[3], 64, 1), v[2])
+        mix_d[at(0), :] = jnp.where(half0, v[2], pltpu.roll(v[3], 64, 1))
+        mix_u[at(0), :] = jnp.where(half0, pltpu.roll(v[3], 64, 1), v[2])
 
     def group(r, carry):
         for i in range(4):
@@ -109,6 +107,13 @@
         return carry
 
     lax.fori_loop(0, ROWS // 32, group, 0)
+    for out, mix in ((down, mix_d), (up, mix_u)):
+        for i in range(3):
+            ref, at = (own, i * ROWS) if i < 2 else (mix, 0)
+            for f in range(7):
+                out[i * FAR + f * 8 : i * FAR + f * 8 + 8, :] = ref[at + f * REACH : at + f * REACH + 8, :]
+                out[i * FAR + 56 + f : i * FAR + 57 + f, :] = ref[at + f * REACH + 8 : at + f * REACH + 9, :]
+            out[i * FAR + 63 : i * FAR + 64, :] = jnp.zeros((1, 128), F32)
 
 
 def main_kernel(pos_ref, stiff_tab, cond_tab, own, east, west, east2, west2, out, a_st, b_st, c_st, t0, t1, raw, co):
@@ -140,17 +145,26 @@
             place(i, get(own, i))
             place(4 + i, swap_x(jnp.where(half0, get(east, 3 - i), get(west, 3 - i))))
             place(8 + i, jnp.where(half0, get(west, i), get(east, i)))
+        for i in range(12, 24):
+            place(i, zero)
+        return carry
+
+    lax.fori_loop(0, ROWS // 8, spread, 0)
+    for q in range(8):
+
+        def put_far(xi, v):
+            if q < 7:
+                raw[pl.ds(q * REACH * PLANE + xi, 8, stride=PLANE), :] = v
+            else:
+                raw[pl.ds(8 * PLANE + xi, 8, stride=REACH * PLANE), :] = v
+
+        e = [east2[i * FAR + q * 8 : i * FAR + q * 8 + 8, :] for i in range(3)]
+        w = [west2[i * FAR + q * 8 : i * FAR + q * 8 + 8, :] for i in range(3)]
+        put_far(12, jnp.where(half0, w[2], e[2]))
+        put_far(13, swap_x(jnp.where(half0, e[2], w[2])))
         for i in range(2):
-            place(14 + i, swap_x(jnp.where(half0, get(east2, 1 - i), get(west2, 1 - i))))
-            place(16 + i, jnp.where(half0, get(west2, i), get(east2, i)))
-        e, w = get(east2, 2), get(west2, 2)
-        place(13, swap_x(jnp.where(half0, e, w)))
-        place(12, jnp.where(half0, w, e))
-        for i in range(6):
-            place(18 + i, zero)
-        return carry
-
-    lax.fori_loop(0, ROWS // 8, spread, 0)
+            put_far(14 + i, swap_x(jnp.where(half0, e[1 - i], w[1 - i])))
+            put_far(16 + i, jnp.where(half0, w[i], e[i]))
 
     x0, z0 = pos_ref[0], pos_ref[1]
 
@@ -230,50 +244,51 @@
         return jnp.where(has_s, pltpu.roll(v, 1, 1), 0.0)
 
     def advance(ref, slot, radius, fine, emit):
-        units = (radius + 5) // 2
+        inner = (radius + 1) // 2
         passes = jnp.where(radius > 12, 2, 1)
 
-        def unit(at, ca, carry):
+        near = [(d * PLANE + 8 * b, b) for d in range(2) for b in range(2)]
+        far = [(d * PLANE, 0) for d in range(4)]
+
+        def unit(at, ca, carry, tiles):
             carry = list(carry)
-            for d in range(2):
-                for b in range(2):
-                    off = d * PLANE + 8 * b
-                    mid = {f: load(ref, at, f, off) for f in MOVED}
-                    e = {f: load(ref, at, f, off + 1) for f in MOVED}
-                    w = {f: load(ref, at, f, off - 1) for f in MOVED}
-                    i = {f: load(ref, at, f, off + PLANE) for f in MOVED}
-                    o = {f: load(ref, at, f, off - PLANE) for f in (0, 1, 2, 3)}
-                    n, s = {}, {}
-                    for j, f in enumerate(MOVED):
-                        n[f] = north(mid[f])
-                        s[f] = south(mid[f])
-                    p, k = mid[3], mid[5]
-                    face = (i[5] + k) * (i[3] - p)
-                    flux = face - carry[b]
-                    carry[b] = face
-                    for side in (e, w, n, s):
-                        flux = flux + (side[5] + k) * (side[3] - p)
-                    dil = (e[0] - w[0]) + (n[1] - s[1]) + (i[2] - o[2])
-                    m = coef(ca, 6, off)
-                    grads = [e[3] - w[3], n[3] - s[3], i[3] - o[3]]
-                    gain = GAIN
-                    if not fine:
-                        m = m * float(FINE)
-                        grads[1] = grads[1] * float(FINE)
-                        flux = flux * float(FINE)
-                        gain = GAIN * FINE
-                    grads[0] = grads[0] * m
-                    grads[2] = grads[2] * m
-                    a = coef(ca, 0 if fine else 2, off)
-                    a6 = coef(ca, 1 if fine else 3, off)
-                    new = []
-                    for f in range(3):
-                        around = (e[f] + w[f]) + (n[f] + s[f]) + (i[f] + o[f])
-                        new.append(a * around + a6 * mid[f] - grads[f])
-                    new.append(coef(ca, 4, off) * (p + (flux - gain * dil)))
-                    psi = load(ref, at, 4, off)
-                    new.append(psi * (1.0 - (dil if fine else dil * float(FINE))))
-                    emit(at - slot * SLOT, ca, off, new)
+            for off, b in tiles:
+                mid = {f: load(ref, at, f, off) for f in MOVED}
+                e = {f: load(ref, at, f, off + 1) for f in MOVED}
+                w = {f: load(ref, at, f, off - 1) for f in MOVED}
+                i = {f: load(ref, at, f, off + PLANE) for f in MOVED}
+                o = {f: load(ref, at, f, off - PLANE) for f in (0, 1, 2, 3)}
+                n, s = {}, {}
+                for j, f in enumerate(MOVED):
+                    n[f] = north(mid[f])
+                    s[f] = south(mid[f])
+                p, k = mid[3], mid[5]
+                face = (i[5] + k) * (i[3] - p)
+                flux = face - carry[b]
+                carry[b] = face
+                for side in (e, w, n, s):
+                    flux = flux + (side[5] + k) * (side[3] - p)
+                dil = (e[0] - w[0]) + (n[1] - s[1]) + (i[2] - o[2])
+                m = coef(ca, 6, off)
+                grads = [e[3] - w[3], n[3] - s[3], i[3] - o[3]]
+                gain = GAIN
+                if not fine:
+                    m = m * float(FINE)
+                    grads[1] = grads[1] * float(FINE)
+                    flux = flux * float(FINE)
+                    gain = GAIN * FINE
+                grads[0] = grads[0] * m
+                grads[2] = grads[2] * m
+                a = coef(ca, 0 if fine else 2, off)
+                a6 = coef(ca, 1 if fine else 3, off)
+                new = []
+                for f in range(3):
+                    around = (e[f] + w[f]) + (n[f] + s[f]) + (i[f] + o[f])
+                    new.append(a * around + a6 * mid[f] - grads[f])
+                new.append(coef(ca, 4, off) * (p + (flux - gain * dil)))
+                psi = load(ref, at, 4, off)
+                new.append(psi * (1.0 - (dil if fine else dil * float(FINE))))
+                emit(at - slot * SLOT, ca, off, new)
             return tuple(carry)
 
         start = where_of(slot, 0)
@@ -313,9 +328,11 @@
                 p0, p1 = load(ref, at, 3, 8 * b - PLANE), load(ref, at, 3, 8 * b)
                 carry.append((k0 + k1) * (p1 - p0))
 
-            def moved(u, carry):
+            units = jnp.where(b0 == 0, inner, 2)
+
+            def moved(u, carry, tiles=near):
                 shift = u * (2 * PLANE)
-                return unit(pl.multiple_of(at + shift, 8), pl.multiple_of(ca + shift, 8), carry)
+                return unit(pl.multiple_of(at + shift, 8), pl.multiple_of(ca + shift, 8), carry, tiles)
 
             def two(u, carry):
                 return moved(2 * u + 1, moved(2 * u, carry))
@@ -324,7 +341,11 @@
 
             @pl.when(units % 2 == 1)
             def _():
-                moved(units - 1, carry)
+                moved(units, moved(units - 1, carry), far)
+
+            @pl.when((units % 2 == 0) & (b0 == 0))
+            def _():
+                moved(units, carry, far)
 
             return c
 
@@ -495,9 +516,10 @@
 def fold(recv):
     return pl.pallas_call(
         fold_kernel,
-        out_shape=(shaped(4 * ROWS), shaped(3 * ROWS), shaped(3 * ROWS)),
+        out_shape=(shaped(4 * ROWS), shaped(3 * FAR), shaped(3 * FAR)),
         in_specs=[vmem()],
         out_specs=(vmem(), vmem(), vmem()),
+        scratch_shapes=[scratch(ROWS), scratch(ROWS)],
         compiler_params=pltpu.CompilerParams(vmem_limit_bytes=8 << 20),
         interpret=INTERPRET,
         name="fold",
@@ -517,7 +539,7 @@
             scratch(7 * SLOT + PAD),
             scratch(SLOT + PAD),
             scratch(SLOT + PAD),
-            scratch(ROWS * PLANE),
+            scratch(ROWS * PLANE + 256),
             scratch(7 * FIELD + PAD),
         ],
         compiler_params=pltpu.CompilerParams(vmem_limit_bytes=42 << 20),

time: 113 us -> 102 us (0.903)
  Pallas kernels: 54.7 us -> 47.2 us
  waiting for transfers between devices: 15.4 us -> 11.3 us
    pallas_call x1, Pallas kernels: 50.8 us -> 43.3 us  [compute(): pl.pallas_call(main_kernel, out_shape=shaped(32 * 20), in_specs=[smem(),...]
    ppermute x4, waiting for transfers between devices: 9.47 us -> 5.38 us  [from_side(): return lax.ppermute(value, 'gx', pairs)]
  transfers between devices with their start and end apart: 5 -> 5, of which waited for: 3 -> 4; matrix products, arithmetic and copies ran while one was open for 0% -> 0% of each run, Pallas kernels for 0% -> 0%
where the time goes in v5:
time: 102 us; the launch traced here: 101 us
  Pallas kernels  47.2 us (46%)
  blocking collectives  22.4 us (22%)
  starting transfers between devices  20.1 us (20%)
  waiting for transfers between devices  11.3 us (11%)
    pallas_call x1, Pallas kernels, compute(): pl.pallas_call(main_kernel, out_shape=shaped(32 * 20), in_specs=[smem(),...  43.3 us
    all_to_all x1, blocking collectives, shards(): lax.all_to_all(ends.reshape(32, 5, 4, 128), ('ta', 'gy'), 0, 0, tiled=True)  22.4 us
    ppermute x4, starting transfers between devices, from_side(): return lax.ppermute(value, 'gx', pairs)  16.7 us
    all_to_all x1, waiting for transfers between devices, shards(): got = lax.all_to_all(sent.reshape(4, ROWS, 128), 'gy', 0, 0, tiled=True)  5.96 us
    ppermute x4, waiting for transfers between devices, from_side(): return lax.ppermute(value, 'gx', pairs)  5.38 us
    all_to_all x1, starting transfers between devices, shards(): got = lax.all_to_all(sent.reshape(4, ROWS, 128), 'gy', 0, 0, tiled=True)  3.41 us
    pallas_call x1, Pallas kernels, pack(): pl.pallas_call(pack_kernel, out_shape=shaped(4 * ROWS), in_specs=[smem()]...  2.05 us
  transfers between devices with their start and end apart: 5, of which 4 were waited for; matrix products, arithmetic and copies ran while one was open for 0% of the time, Pallas kernels for 0%

profile of v5, /device:TPU:6, one launch (start us, length us, event | category | flops | bytes accessed | tf_op | source)
XLA Modules:
  0.0 101.3 jit_solution(3938673860966606462)
XLA Ops:
  0.0 2.0 %pack.1 = f32[512,128]{1,0:T(8,128)} custom-call(s32[1]{0:T(128)} %bitcast.2.ta_ref, f32[3,64,256]{2,1,0:T(8,128)} %bitcast.17, f32[64,256]{1,0:T(8,128)} %bitcast.18, f32[64,256]{1,0:T(8,128)} %bitcast.19, s32[64,256]{1,0:T(8,128)} %bitcast.20, s32[64,256]{1,0:T(8,128)} %bitcast.21), custom_call_target="tpu_custom_call" | custom-call | tf_op jit(solution)/shard_map/pack/pallas_call | solution.py:505
  2.0 3.4 %all-to-all-start = ((f32[4,128,128]{2,1,0:T(8,128)}), f32[4,128,128]{2,1,0:T(8,128)S(1)}, u32[]{:S(2)}, u32[]{:S(2)}) async-start(f32[4,128,128]{2,1,0:T(8,128)} %bitcast.16), calls=%async_computation | async-start | bytes 524288 | tf_op jit(solution)/shard_map/all_to_all | solution.py:570
  5.5 6.0 %all-to-all-done = f32[4,128,128]{2,1,0:T(8,128)S(1)} async-done(((f32[4,128,128]{2,1,0:T(8,128)}), f32[4,128,128]{2,1,0:T(8,128)S(1)}, u32[]{:S(2)}, u32[]{:S(2)}) %all-to-all-start) | async-done | bytes 262176 | tf_op jit(solution)/shard_map/all_to_all | solution.py:570
  11.4 0.9 fold.1
  12.3 0.0 copy-start.1
  12.3 5.0 %collective-permute-start.1 = (f32[512,128]{1,0:T(8,128)S(1)}, f32[512,128]{1,0:T(8,128)S(1)}, u32[]{:S(2)}, u32[]{:S(2)}) collective-permute-start(f32[512,128]{1,0:T(8,128)S(1)} %get-tuple-element.8.own), channel_id=1, source_target_pairs={{0,32},{32,64},{64,96},{96,128},{128,160},{160,192},{192,224},{1,3... | collective-permute-start | bytes 786440 | tf_op jit(solution)/shard_map/ppermute | solution.py:575
  17.4 1.9 %collective-permute-start = (f32[512,128]{1,0:T(8,128)S(1)}, f32[512,128]{1,0:T(8,128)S(1)}, u32[]{:S(2)}, u32[]{:S(2)}) collective-permute-start(f32[512,128]{1,0:T(8,128)S(1)} %get-tuple-element.8.own), channel_id=1, source_target_pairs={{32,0},{64,32},{96,64},{128,96},{160,128},{192,160},{224,192},{33,... | collective-permute-start | bytes 786440 | tf_op jit(solution)/shard_map/ppermute | solution.py:575
  19.3 0.0 copy-done.1
  19.3 2.2 %collective-permute-start.2 = (f32[192,128]{1,0:T(8,128)S(1)}, f32[192,128]{1,0:T(8,128)S(1)}, u32[]{:S(2)}, u32[]{:S(2)}) collective-permute-start(f32[192,128]{1,0:T(8,128)S(1)} %get-tuple-element.9), channel_id=1, source_target_pairs={{64,0},{96,32},{128,64},{160,96},{192,128},{224,160},{65,1},{97,33... | collective-permute-start | bytes 294920 | tf_op jit(solution)/shard_map/ppermute | solution.py:575
  21.5 7.5 %collective-permute-start.3 = (f32[192,128]{1,0:T(8,128)S(1)}, f32[192,128]{1,0:T(8,128)S(1)}, u32[]{:S(2)}, u32[]{:S(2)}) collective-permute-start(f32[192,128]{1,0:T(8,128)S(1)} %get-tuple-element.10), channel_id=1, source_target_pairs={{0,64},{32,96},{64,128},{96,160},{128,192},{160,224},{1,65},{33,97... | collective-permute-start | bytes 294920 | tf_op jit(solution)/shard_map/ppermute | solution.py:575
  29.1 0.0 copy-start
  29.1 0.1 pad_add_fusion.pos_ref
  29.2 1.6 %collective-permute-done.2.east2 = f32[192,128]{1,0:T(8,128)S(1)} collective-permute-done((f32[192,128]{1,0:T(8,128)S(1)}, f32[192,128]{1,0:T(8,128)S(1)}, u32[]{:S(2)}, u32[]{:S(2)}) %collective-permute-start.2) | collective-permute-done | bytes 98336 | tf_op jit(solution)/shard_map/ppermute | solution.py:575
  30.7 0.5 collective-permute-done.3.west2
  31.3 0.0 collective-permute-done.1.west
  31.3 3.3 %collective-permute-done.east = f32[512,128]{1,0:T(8,128)S(1)} collective-permute-done((f32[512,128]{1,0:T(8,128)S(1)}, f32[512,128]{1,0:T(8,128)S(1)}, u32[]{:S(2)}, u32[]{:S(2)}) %collective-permute-start) | collective-permute-done | bytes 262176 | tf_op jit(solution)/shard_map/ppermute | solution.py:575
  34.5 0.0 copy-done
  34.5 43.3 %parareal.1 = f32[640,128]{1,0:T(8,128)S(1)} custom-call(s32[2]{0:T(128)S(1)} %pad_add_fusion.pos_ref, f32[6]{0:T(128)S(1)} %copy-done, f32[6]{0:T(128)S(1)} %multiply_add_fusion.cond_tab, f32[512,128]{1,0:T(8,128)S(1)} %get-tuple-element.8.own, f32[512,128]{1,0:T(8,128)S(1)} %collective-permute-done.east, f32[512,128]{1,0:T(8,128)S(1)} %collective-permute-done.1.west, ...), custom_call_target="tpu_custom_call" | custom-call | tf_op jit(solution)/shard_map/parareal/pallas_call | solution.py:531
  77.8 22.4 %all_to_all.10 = f32[32,5,4,128]{3,2,1,0:T(4,128)S(1)} all-to-all(f32[32,5,4,128]{3,2,1,0:T(4,128)S(1)} %bitcast.14), channel_id=1, replica_groups=mesh['gx'=8,'gy'=4,'ta'=8] {'ta','gy'}, dimensions={0} | all-to-all | bytes 655360 | tf_op jit(solution)/shard_map/all_to_all | solution.py:579
  100.3 1.0 unpack.1
  (1 shorter events, 0.0 us)
Async XLA Ops:
  2.0 9.4 %all-to-all-start = ((f32[4,128,128]{2,1,0:T(8,128)}), f32[4,128,128]{2,1,0:T(8,128)S(1)}, u32[]{:S(2)}, u32[]{:S(2)}) async-start(f32[4,128,128]{2,1,0:T(8,128)} %bitcast.16), calls=%async_computation | async-start | bytes 524288 | tf_op jit(solution)/shard_map/all_to_all | solution.py:570
  12.3 7.0 %copy-start.1 = (f32[6]{0:T(128)S(1)}, f32[6]{0:T(128)}, u32[]{:S(2)}) copy-start(f32[6]{0:T(128)} %param.13) | copy-start | bytes 76
  12.3 18.9 %collective-permute-start.1 = (f32[512,128]{1,0:T(8,128)S(1)}, f32[512,128]{1,0:T(8,128)S(1)}, u32[]{:S(2)}, u32[]{:S(2)}) collective-permute-start(f32[512,128]{1,0:T(8,128)S(1)} %get-tuple-element.8.own), channel_id=1, source_target_pairs={{0,32},{32,64},{64,96},{96,128},{128,160},{160,192},{192,224},{1,3... | collective-permute-start | bytes 786440 | tf_op jit(solution)/shard_map/ppermute | solution.py:575
  17.4 17.2 %collective-permute-start = (f32[512,128]{1,0:T(8,128)S(1)}, f32[512,128]{1,0:T(8,128)S(1)}, u32[]{:S(2)}, u32[]{:S(2)}) collective-permute-start(f32[512,128]{1,0:T(8,128)S(1)} %get-tuple-element.8.own), channel_id=1, source_target_pairs={{32,0},{64,32},{96,64},{128,96},{160,128},{192,160},{224,192},{33,... | collective-permute-start | bytes 786440 | tf_op jit(solution)/shard_map/ppermute | solution.py:575
  19.3 11.4 %collective-permute-start.2 = (f32[192,128]{1,0:T(8,128)S(1)}, f32[192,128]{1,0:T(8,128)S(1)}, u32[]{:S(2)}, u32[]{:S(2)}) collective-permute-start(f32[192,128]{1,0:T(8,128)S(1)} %get-tuple-element.9), channel_id=1, source_target_pairs={{64,0},{96,32},{128,64},{160,96},{192,128},{224,160},{65,1},{97,33... | collective-permute-start | bytes 294920 | tf_op jit(solution)/shard_map/ppermute | solution.py:575
  21.5 9.7 %collective-permute-start.3 = (f32[192,128]{1,0:T(8,128)S(1)}, f32[192,128]{1,0:T(8,128)S(1)}, u32[]{:S(2)}, u32[]{:S(2)}) collective-permute-start(f32[192,128]{1,0:T(8,128)S(1)} %get-tuple-element.10), channel_id=1, source_target_pairs={{0,64},{32,96},{64,128},{96,160},{128,192},{160,224},{1,65},{33,97... | collective-permute-start | bytes 294920 | tf_op jit(solution)/shard_map/ppermute | solution.py:575
  29.1 5.5 %copy-start = (f32[6]{0:T(128)S(1)}, f32[6]{0:T(128)}, u32[]{:S(2)}) copy-start(f32[6]{0:T(128)} %stiff_tab.1) | copy-start | bytes 76
